TPU v7x, 32 devices: a whole 2x2x4 slice. The times are simulated.
32 devices in a mesh: dp: 16 (over z, x, core), shard: 2 (over y).
Axes of the slice: x: 2, y: 2, z: 4, core: 2. Of those that a mesh axis runs over, the one named last changes fastest.
Arguments:
- acts: bfloat16 [32768, 4096], P('dp', 'shard'), may hold values from -6 to 6
- grad_out: bfloat16 [32768, 14336], P('dp', 'shard'), may hold values from -15 to 15
- projector: bfloat16 [4096, 512], P('shard'), may hold values from -0.09375 to 0.09375
- weight: bfloat16 [4096, 14336], P('dp', 'shard'), may hold values from -0.09375 to 0.09375
- moment1: float32 [512, 14336], P('dp', 'shard'), may hold values from -24 to 24
- moment2: float32 [512, 14336], P('dp', 'shard'), may hold values from 1 to 16
Outputs:
- new_weight: bfloat16 [4096, 14336], P('dp', 'shard')
- new_moment1: float32 [512, 14336], P('dp', 'shard')
- new_moment2: float32 [512, 14336], P('dp', 'shard')
All inputs are finite; a program needn't handle non-finite values.
Results may differ from a plain program's by a relative error of at most 0.005.
Values may be sent and summed in bfloat16 or wider, within the bound.
No kernel may reach another device: no remote copies, remote signals or barrier semaphores. Data moves between devices by JAX's collectives and lax.ppermute only.
A program may use at most 128 MiB of HBM per device.

v0:
```python
import functools

import jax
import jax.numpy as jnp
from jax import lax
from jax.experimental import pallas as pl
from jax.experimental.pallas import tpu as pltpu
from jax.sharding import PartitionSpec as P


first_fix = 0.9999734386011124
second_fix = 0.994079470779666
PROJECTION_TILE = 512
LAST_UNITS = 14
RANK_PARTS = (1, 2, 1)
COLUMN_PARTS = (1, 2, 2)
UPDATE_PARTS = (3, 3, 1)
LAST_ORDER = (0, 1, 2)
PIPELINE = (
    (0, 0), (0, 1), (1, 0), (0, 2), (1, 1), (2, 0), (0, 3), (3, 0),
    (2, 1), (4, 0), (3, 1), (1, 2), (4, 1), (0, 4), (2, 2), (1, 3),
    (3, 2), (4, 2), (2, 3), (1, 4), (3, 3), (4, 3), (2, 4), (3, 4),
    (4, 4),
)
F32 = jnp.float32
BF16 = jnp.bfloat16


def flip_pairs(n, bits):
    return [(i, i ^ bits) for i in range(n)]


def chunk_count(units, wanted):
    while units % wanted:
        wanted -= 1
    return wanted


def selection(rank, source):
    rows = lax.broadcasted_iota(jnp.int32, (rank, source.shape[0]), 0)
    return (rows == source[None, :]).astype(BF16)


def last_kernel(groups, basis_ref, *refs):
    parts, weight_ref, out_ref = refs[:groups], refs[groups], refs[-1]
    change = None
    update = jnp.concatenate([part[...] for part in parts], axis=0)
    change = jnp.dot(basis_ref[...], update, preferred_element_type=F32)
    out_ref[...] = (weight_ref[...].astype(F32) - 0.2 * change).astype(BF16)


def last_product(basis, parts, weight, before, start, width):
    rows, columns = weight.shape
    tile = chunk_tile(width, LAST_UNITS)
    first = start // tile
    part_specs = [pl.BlockSpec((p.shape[0], tile), lambda i: (0, i)) for p in parts]
    there = pl.BlockSpec((rows, tile), lambda i: (0, i + first))
    in_specs = [pl.BlockSpec(basis.shape, lambda i: (0, 0)), *part_specs, there]
    args = [basis, *parts, weight]
    aliases = {}
    if before is not None:
        in_specs.append(pl.BlockSpec(memory_space=pl.ANY))
        aliases = {len(args): 0}
        args.append(before)
    return pl.pallas_call(
        functools.partial(last_kernel, len(parts)),
        grid=(width // tile,),
        in_specs=in_specs,
        out_specs=there,
        out_shape=jax.ShapeDtypeStruct((rows, columns), BF16),
        input_output_aliases=aliases,
    )(*args)


def chunk_tile(width, most):
    units = width // 128
    best = 1
    for n in range(1, most + 1):
        if units % n == 0:
            best = n
    return best * 128


def from_root(block, axis, holder):
    block = jnp.where(lax.axis_index(axis) == holder, block, jnp.zeros_like(block))
    return lax.psum(block, axis)


def projection_kernel(counts, pick_ref, projector_ref, acts_ref, *refs):
    outs, picked = refs[:-1], refs[-1]

    @pl.when(pl.program_id(0) == 0)
    def _():
        picked[...] = lax.dot_general(
            pick_ref[...],
            projector_ref[...],
            (((1,), (1,)), ((), ())),
            preferred_element_type=F32,
        ).astype(BF16)

    part = lax.dot_general(
        picked[...], acts_ref[...], (((1,), (1,)), ((), ())), preferred_element_type=F32
    )
    first = 0
    for i, n in enumerate(counts):
        outs[2 * i][...] = part[first : first + n]
        outs[2 * i + 1][...] = part[first : first + n].astype(BF16)
        first += n


def projections(pick, projector, acts, counts, part=0, of=1):
    tokens, features = acts.shape[0] // of, acts.shape[1]
    tile = min(PROJECTION_TILE, tokens)
    first = part * (tokens // tile)
    shapes, specs = [], []
    for n in counts:
        for dtype in (F32, BF16):
            shapes.append(jax.ShapeDtypeStruct((n, tokens), dtype))
            specs.append(pl.BlockSpec((n, tile), lambda i: (0, i)))
    outs = pl.pallas_call(
        functools.partial(projection_kernel, counts),
        grid=(tokens // tile,),
        in_specs=[
            pl.BlockSpec(pick.shape, lambda i: (0, 0), pipeline_mode=pl.Buffered(1)),
            pl.BlockSpec(projector.shape, lambda i: (0, 0), pipeline_mode=pl.Buffered(1)),
            pl.BlockSpec((tile, features), lambda i: (i + first, 0)),
        ],
        out_specs=specs,
        out_shape=shapes,
        scratch_shapes=[pltpu.VMEM((pick.shape[0], features), BF16)],
    )(pick, projector, acts)
    return list(zip(outs[::2], outs[1::2]))


def halve(kept, received):
    total = kept + received.astype(F32)
    half = total.shape[0] // 2
    return total[:half], total[half:].astype(BF16)


def gradient_part(projected, grad_out, start, width):
    half = projected.shape[0] // 2
    part = jnp.dot(
        projected, grad_out[:, start : start + width], preferred_element_type=F32
    )
    return part[:half], part[half:].astype(BF16)


def after(value, *others):
    return lax.optimization_barrier((value, *others))[0] if others else value


def body(dp, shard, acts, grad_out, projector, weight, moment1, moment2):
    rank = projector.shape[1]
    columns = grad_out.shape[1]
    own_rows = rank // dp
    depth = dp // 4
    bits = dp.bit_length() - 1
    me = lax.axis_index("dp")
    pairs = [flip_pairs(dp, 1 << b) for b in range(bits)]
    place = jnp.arange(dp, dtype=jnp.int32)
    owner = me ^ sum(((place >> (bits - 1 - b)) & 1) << b for b in range(bits))

    def hop(value, stage):
        return lax.ppermute(value, "dp", pairs[stage])

    def fetch(part, sent):
        if shard == 2:
            return lax.ppermute(sent, "shard", [(0, 1), (1, 0)])
        share = lax.psum_scatter(part, "shard", scatter_dimension=1, tiled=True).astype(BF16)
        return lax.all_gather(share, "shard", axis=1, tiled=True)

    def complete(own, other, gate):
        other = after(other, *gate)
        return other if shard > 2 else (own + other.astype(F32)).astype(BF16)

    parts, splits = RANK_PARTS, COLUMN_PARTS
    if own_rows % sum(parts) or own_rows // sum(parts) < 8:
        parts, splits = (1,), (2,)
    unit_rows = own_rows // sum(parts)
    sources = []
    first = 0
    for n in parts:
        rows = owner[:, None] * own_rows + first + jnp.arange(n * unit_rows)[None, :]
        sources.append(rows.reshape(-1))
        first += n * unit_rows

    def one_hot(source):
        columns_at = lax.broadcasted_iota(jnp.int32, (source.shape[0], rank), 1)
        return (source[:, None] == columns_at).astype(BF16)

    halves = 1
    firsts, token = [], []
    for h in range(halves):
        pick = after(one_hot(sources[0]), *token)
        firsts += projections(pick, projector, acts, [sources[0].shape[0]], h, halves)
        token = firsts[-1]
    parts_sent = [firsts[0]]
    if len(sources) > 1:
        rest = after(one_hot(jnp.concatenate(sources[1:])), *token)
        parts_sent += projections(rest, projector, acts, [r.shape[0] for r in sources[1:]])

    weight_rows = weight.shape[0]
    basis_count = projector.shape[0]
    holder = me * weight_rows // basis_count
    offset = me * weight_rows - holder * basis_count
    candidate = lax.dynamic_slice_in_dim(projector, offset, weight_rows, 0)
    swapped = candidate
    if shard == 2:
        swapped = lax.ppermute(candidate, "shard", [(0, 1), (1, 0)])

    def own_basis(ready):
        if shard == 2:
            mine, theirs = lax.optimization_barrier((candidate, swapped, ready))[:2]
            basis = jnp.where(lax.axis_index("shard") == holder, mine, theirs)
        else:
            basis = from_root(candidate, "shard", holder)

        def z_before(s):
            return (me // 4 + depth - s) % depth * 4 + me % 4

        order_z = jnp.stack([z_before(s) for s in range(depth)])
        later = jnp.concatenate(
            [jnp.stack([order_z ^ c, order_z ^ (2 + c)], axis=1).reshape(-1) for c in (0, 1)]
        )
        order = (later[:, None] * own_rows + jnp.arange(own_rows)[None, :]).reshape(-1)
        return jnp.dot(basis, selection(rank, order), preferred_element_type=F32).astype(BF16)

    units = []
    for chunk, n in enumerate(parts):
        pieces = chunk_count(columns // 128, splits[chunk])
        for p in range(pieces):
            units.append((chunk, p * (columns // pieces), columns // pieces))
    fetched = [fetch(*part) for part in firsts]
    fetched = [fetched] + [[fetch(*p)] for i, p in enumerate(parts_sent) if i]
    parts_own = [[p[0] for p in firsts]] + [[p[0]] for p in parts_sent[1:]]
    steps = PIPELINE
    if len(units) != 5 or bits != 4:
        steps = [(i, stage) for i in range(len(units)) for stage in range(bits + 1)]
    sums, state, gate = {}, {}, [p for pair in parts_sent[1:] for p in pair]
    for i, stage in steps:
        if stage == 0:
            chunk, start, width = units[i]
            if chunk not in sums:
                both = zip(parts_own[chunk], fetched[chunk])
                sums[chunk] = jnp.concatenate([complete(a, b, gate) for a, b in both], axis=1)
                gate = []
            kept, sent = gradient_part(after(sums[chunk], *gate), grad_out, start, width)
            if i == len(units) - 1:
                basis = own_basis(sent)
        else:
            kept, received = state[i]
            if (i, stage) == steps[-2]:
                gate.append(basis)
            received = after(received, *gate)
            if stage == bits:
                state[i] = kept + received.astype(F32)
                gate = [state[i]]
                continue
            kept, sent = halve(kept, received)
        gate = [sent]
        state[i] = (kept, hop(sent, stage))
    done = [state[i] for i in range(len(units))]
    rows = []
    for chunk in range(len(parts)):
        rows.append(jnp.concatenate([d for d, u in zip(done, units) if u[0] == chunk], axis=1))
    gradient = jnp.concatenate(rows, axis=0)

    squares = jnp.sum(gradient * gradient).reshape(1, 1)
    squares = jnp.broadcast_to(squares, (8, 128))
    devices = dp * shard
    if shard == 2:
        everywhere = jnp.broadcast_to(squares[None], (devices, 8, 128))
        squares = lax.all_to_all(everywhere, ("dp", "shard"), 0, 0, tiled=True).sum(0)
    else:
        squares = lax.psum(squares, ("dp", "shard"))
    square_sum = squares[0, 0]
    whole = rank * columns * shard
    root_mean = jnp.sqrt(square_sum / whole + 1e-06)
    clip_factor = jnp.minimum(1.0, 4.0 / root_mean)

    clipped = clip_factor * gradient
    new_moment1 = 0.9 * moment1 + 0.1 * clipped
    new_moment2 = 0.95 * moment2 + 0.05 * clipped * clipped
    update = (new_moment1 / first_fix / (jnp.sqrt(new_moment2 / second_fix) + 1e-08)).astype(BF16)

    ring = [(i, (i + 4) % dp) for i in range(dp)]
    new_weight = None
    shares = UPDATE_PARTS if columns % (128 * sum(UPDATE_PARTS)) == 0 else (1,)
    for j, share in sorted(enumerate(shares), key=lambda part: LAST_ORDER[part[0]]):
        start = columns // sum(shares) * sum(shares[:j])
        width = columns // sum(shares) * share
        mine = update[:, start : start + width]
        blocks = []
        if j == 2:
            other = hop(mine, 1)
            blocks.append(jnp.concatenate([mine, other], axis=0))
            for _ in range(1, depth):
                blocks.append(lax.ppermute(blocks[-1], "dp", ring))
        else:
            for s in range(depth):
                if s:
                    mine = lax.ppermute(mine, "dp", ring)
                blocks += [mine, hop(mine, 1)]
        for block in list(blocks):
            blocks.append(hop(block, 0))
        new_weight = last_product(basis, blocks, weight, new_weight, start, width)
    return (new_weight, new_moment1, new_moment2)


def solution(mesh):
    dp, shard = mesh.shape["dp"], mesh.shape["shard"]

    def step(*args):
        return body(dp, shard, *args)

    return jax.shard_map(
        step,
        mesh=mesh,
        in_specs=(
            P("dp", "shard"),
            P("dp", "shard"),
            P("shard", None),
            P("dp", "shard"),
            P("dp", "shard"),
            P("dp", "shard"),
        ),
        out_specs=(P("dp", "shard"), P("dp", "shard"), P("dp", "shard")),
        check_vma=False,
    )
```

profile of v0, /device:TPU:0, one launch (start us, length us, event | category | flops | bytes accessed | tf_op | source)
XLA Modules:
  0.0 203.7 jit_solution(5370632230178734951)
XLA Ops:
  0.8 0.8 fusion.13.pick_ref
  1.6 8.2 %shard_map.85 = (f32[128,2048]{1,0:T(8,128)}, bf16[128,2048]{1,0:T(8,128)(2,1)}) custom-call(bf16[128,512]{1,0:T(8,128)(2,1)} %fusion.13.pick_ref, bf16[2048,512]{1,0:T(8,128)(2,1)} %projector_ref.3, bf16[2048,2048]{1,0:T(8,128)(2,1)} %acts_ref.3), custom_call_target="tpu_custom_call" | custom-call | tf_op jit(solution)/shard_map/pallas_call | solution.py:120
  9.8 3.0 %collective-permute-start.2 = (bf16[128,2048]{1,0:T(8,128)(2,1)}, bf16[128,2048]{1,0:T(8,128)(2,1)S(1)}, u32[]{:S(2)}, u32[]{:S(2)}) collective-permute-start(bf16[128,2048]{1,0:T(8,128)(2,1)} %get-tuple-element.38), channel_id=1, source_target_pairs={{0,1},{1,0},{2,3},{3,2},{4,5},{5,4},{6,7},{7,6},{8,9},{9,8},{10,11... | collective-permute-start | bytes 1572872 | tf_op jit(solution)/shard_map/ppermute | solution.py:169
  13.1 0.9 fusion.9.pick_ref
  14.0 9.7 %shard_map.86 = (f32[256,2048]{1,0:T(8,128)}, bf16[256,2048]{1,0:T(8,128)(2,1)}, f32[128,2048]{1,0:T(8,128)}, bf16[128,2048]{1,0:T(8,128)(2,1)}) custom-call(bf16[384,512]{1,0:T(8,128)(2,1)} %fusion.9.pick_ref, bf16[2048,512]{1,0:T(8,128)(2,1)} %projector_ref.3, bf16[2048,2048]{1,0:T(8,128)(2,1)} %acts_ref.3), custom_call_target="tpu_custom_call" | custom-call | tf_op jit(solution)/shard_map/pallas_call | solution.py:120
  23.7 2.0 collective-permute-start.1
  25.7 1.0 constant_dynamic-slice_fusion
  26.9 11.5 %fusion.10 = f32[128,7168]{1,0:T(8,128)S(1)} fusion(bf16[2048,7168]{1,0:T(8,128)(2,1)} %param.7, f32[128,2048]{1,0:T(8,128)S(1)} %copy-done.2, bf16[128,2048]{1,0:T(8,128)(2,1)S(1)} %collective-permute-done.2), kind=kOutput, calls=%fused_computation.37 | convolution fusion | flops 3758882816 | bytes 34603008 | tf_op jit(solution)/shard_map/dot_general | solution.py:143
  38.4 1.8 copy-done
  40.2 1.0 slice.299
  42.0 2.0 collective-permute-done.3
  44.0 1.9 slice_add_fusion.2
  46.0 1.9 collective-permute-start.4
  47.9 2.0 collective-permute-done.5
  50.3 7.3 %fusion.6 = f32[256,3584]{1,0:T(8,128)S(1)} fusion(bf16[256,2048]{1,0:T(8,128)(2,1)S(1)} %add_convert_fusion, bf16[2048,7168]{1,0:T(8,128)(2,1)} %param.7), kind=kOutput, calls=%fused_computation.6 | convolution fusion | flops 3758096384 | bytes 19398656 | tf_op jit(solution)/shard_map/dot_general | solution.py:143
  57.8 1.0 collective-permute-done.4
  58.8 1.9 collective-permute-start.6
  61.0 1.6 collective-permute-start.11
  62.5 7.3 %fusion.2 = f32[256,3584]{1,0:T(8,128)S(1)} fusion(bf16[256,2048]{1,0:T(8,128)(2,1)S(1)} %add_convert_fusion, bf16[2048,7168]{1,0:T(8,128)(2,1)} %param.7), kind=kOutput, calls=%fused_computation.2 | convolution fusion | flops 3758096384 | bytes 19398656 | tf_op jit(solution)/shard_map/dot_general | solution.py:143
  70.1 2.6 %collective-permute-start.9 = (bf16[8,7168]{1,0:T(8,128)(2,1)S(1)}, bf16[8,7168]{1,0:T(8,128)(2,1)S(1)}, u32[]{:S(2)}, u32[]{:S(2)}) collective-permute-start(bf16[8,7168]{1,0:T(8,128)(2,1)S(1)} %slice.314), channel_id=1, source_target_pairs={{0,16},{2,18},{4,20},{6,22},{8,24},{10,26},{12,28},{14,30},{16,0},... | collective-permute-start | bytes 344072 | tf_op jit(solution)/shard_map/ppermute | solution.py:165
  72.8 1.2 add_convert_fusion.1
  74.0 6.4 %fusion.4 = f32[128,3584]{1,0:T(8,128)S(1)} fusion(bf16[128,2048]{1,0:T(8,128)(2,1)S(1)} %add_convert_fusion.1, bf16[2048,7168]{1,0:T(8,128)(2,1)} %param.7), kind=kOutput, calls=%fused_computation.4 | convolution fusion | flops 1879048192 | bytes 17039360 | tf_op jit(solution)/shard_map/dot_general | solution.py:143
  81.5 6.4 %fusion = f32[128,3584]{1,0:T(8,128)S(1)} fusion(bf16[128,2048]{1,0:T(8,128)(2,1)S(1)} %add_convert_fusion.1, bf16[2048,7168]{1,0:T(8,128)(2,1)} %param.7), kind=kOutput, calls=%fused_computation | convolution fusion | flops 1879048192 | bytes 17039360 | tf_op jit(solution)/shard_map/dot_general | solution.py:143
  88.2 1.6 collective-permute-start.18
  89.8 1.1 collective-permute-start.13
  91.0 1.1 convolution_convert_fusion.basis_ref
  92.8 1.6 collective-permute-done.14
  94.5 1.1 collective-permute-start.16
  95.6 2.8 %collective-permute-done.13 = bf16[32,3584]{1,0:T(8,128)(2,1)S(1)} collective-permute-done((bf16[32,3584]{1,0:T(8,128)(2,1)S(1)}, bf16[32,3584]{1,0:T(8,128)(2,1)S(1)}, u32[]{:S(2)}, u32[]{:S(2)}) %collective-permute-start.13) | collective-permute-done | bytes 229408 | tf_op jit(solution)/shard_map/ppermute | solution.py:165
  98.4 0.9 collective-permute-start.15
  99.5 1.1 collective-permute-start.21
  100.6 2.9 %collective-permute-done.17 = bf16[32,3584]{1,0:T(8,128)(2,1)S(1)} collective-permute-done((bf16[32,3584]{1,0:T(8,128)(2,1)S(1)}, bf16[32,3584]{1,0:T(8,128)(2,1)S(1)}, u32[]{:S(2)}, u32[]{:S(2)}) %collective-permute-start.17) | collective-permute-done | bytes 229408 | tf_op jit(solution)/shard_map/ppermute | solution.py:165
  103.6 1.1 collective-permute-start.20
  104.7 0.8 collective-permute-done.16
  106.0 3.4 %collective-permute-done.21 = bf16[16,3584]{1,0:T(8,128)(2,1)S(1)} collective-permute-done((bf16[16,3584]{1,0:T(8,128)(2,1)S(1)}, bf16[16,3584]{1,0:T(8,128)(2,1)S(1)}, u32[]{:S(2)}, u32[]{:S(2)}) %collective-permute-start.21) | collective-permute-done | bytes 114720 | tf_op jit(solution)/shard_map/ppermute | solution.py:165
  109.6 2.1 %collective-permute-done.20 = bf16[16,3584]{1,0:T(8,128)(2,1)S(1)} collective-permute-done((bf16[16,3584]{1,0:T(8,128)(2,1)S(1)}, bf16[16,3584]{1,0:T(8,128)(2,1)S(1)}, u32[]{:S(2)}, u32[]{:S(2)}) %collective-permute-start.20) | collective-permute-done | bytes 114720 | tf_op jit(solution)/shard_map/ppermute | solution.py:165
  111.7 0.9 collective-permute-start.23
  112.6 4.2 %collective-permute-done.19 = bf16[16,3584]{1,0:T(8,128)(2,1)S(1)} collective-permute-done((bf16[16,3584]{1,0:T(8,128)(2,1)S(1)}, bf16[16,3584]{1,0:T(8,128)(2,1)S(1)}, u32[]{:S(2)}, u32[]{:S(2)}) %collective-permute-start.19) | collective-permute-done | bytes 114720 | tf_op jit(solution)/shard_map/ppermute | solution.py:165
  116.8 0.7 collective-permute-done.22
  118.2 0.8 multiply_reduce_fusion
  119.7 10.9 %all_to_all.5 = f32[32,8,128]{2,1,0:T(8,128)S(1)} all-to-all(f32[32,8,128]{2,1,0:T(8,128)S(1)} %broadcast_in_dim_broadcast_in_dim_broadcast_in_dim.2), channel_id=1, replica_groups=mesh['dp'=16,'shard'=2] {'dp','shard'}, dimensions={0} | all-to-all | bytes 262144 | tf_op jit(solution)/shard_map/all_to_all | solution.py:274
  131.9 1.8 divide_convert_fusion
  133.9 0.7 collective-permute-start.47
  134.6 1.4 collective-permute-start.24
  136.0 0.7 collective-permute-start.33
  136.7 5.3 %collective-permute-done.24 = bf16[32,1024]{1,0:T(8,128)(2,1)S(1)} collective-permute-done((bf16[32,1024]{1,0:T(8,128)(2,1)S(1)}, bf16[32,1024]{1,0:T(8,128)(2,1)S(1)}, u32[]{:S(2)}, u32[]{:S(2)}) %collective-permute-start.24) | collective-permute-done | bytes 65568 | tf_op jit(solution)/shard_map/ppermute | solution.py:165
  142.0 0.7 collective-permute-start.32
  143.2 1.4 collective-permute-start.50
  144.6 6.6 %collective-permute-done.25.refs_1_ = bf16[64,1024]{1,0:T(8,128)(2,1)} collective-permute-done((bf16[64,1024]{1,0:T(8,128)(2,1)S(1)}, bf16[64,1024]{1,0:T(8,128)(2,1)}, u32[]{:S(2)}, u32[]{:S(2)}) %collective-permute-start.25) | collective-permute-done | bytes 131104 | tf_op jit(solution)/shard_map/ppermute | solution.py:299
  151.2 0.9 collective-permute-start.49
  152.7 5.6 %collective-permute-done.26.refs_2_ = bf16[64,1024]{1,0:T(8,128)(2,1)} collective-permute-done((bf16[64,1024]{1,0:T(8,128)(2,1)}, bf16[64,1024]{1,0:T(8,128)(2,1)}, u32[]{:S(2)}, u32[]{:S(2)}) %collective-permute-start.26) | collective-permute-done | bytes 131104 | tf_op jit(solution)/shard_map/ppermute | solution.py:299
  158.3 0.9 collective-permute-start.34
  159.8 7.1 %collective-permute-done.35.refs_4_ = bf16[32,3072]{1,0:T(8,128)(2,1)S(1)} collective-permute-done((bf16[32,3072]{1,0:T(8,128)(2,1)S(1)}, bf16[32,3072]{1,0:T(8,128)(2,1)S(1)}, u32[]{:S(2)}, u32[]{:S(2)}) %collective-permute-start.35) | collective-permute-done | bytes 196640 | tf_op jit(solution)/shard_map/ppermute | solution.py:303
  166.9 0.7 collective-permute-start.51
  168.1 1.7 collective-permute-done.27.refs_3_
  169.8 6.1 %collective-permute-done.52.refs_6_ = bf16[32,3072]{1,0:T(8,128)(2,1)S(1)} collective-permute-done((bf16[32,3072]{1,0:T(8,128)(2,1)S(1)}, bf16[32,3072]{1,0:T(8,128)(2,1)S(1)}, u32[]{:S(2)}, u32[]{:S(2)}) %collective-permute-start.52) | collective-permute-done | bytes 196640 | tf_op jit(solution)/shard_map/ppermute | solution.py:303
  176.5 1.9 collective-permute-start.53
  178.6 5.1 %collective-permute-done.36.refs_5_ = bf16[32,3072]{1,0:T(8,128)(2,1)S(1)} collective-permute-done((bf16[32,3072]{1,0:T(8,128)(2,1)S(1)}, bf16[32,3072]{1,0:T(8,128)(2,1)S(1)}, u32[]{:S(2)}, u32[]{:S(2)}) %collective-permute-start.36) | collective-permute-done | bytes 196640 | tf_op jit(solution)/shard_map/ppermute | solution.py:165
  184.3 3.5 %collective-permute-done.53.refs_7_ = bf16[32,3072]{1,0:T(8,128)(2,1)S(1)} collective-permute-done((bf16[32,3072]{1,0:T(8,128)(2,1)S(1)}, bf16[32,3072]{1,0:T(8,128)(2,1)S(1)}, u32[]{:S(2)}, u32[]{:S(2)}) %collective-permute-start.53) | collective-permute-done | bytes 196640 | tf_op jit(solution)/shard_map/ppermute | solution.py:165
  188.3 1.6 collective-permute-done.38.refs_7_
  191.2 0.7 copy-done.38
  191.9 4.0 %shard_map.87.refs_17_ = bf16[256,7168]{1,0:T(8,128)(2,1)} custom-call(bf16[256,512]{1,0:T(8,128)(2,1)} %convolution_convert_fusion.basis_ref, bf16[32,3072]{1,0:T(8,128)(2,1)} %copy-done.7, bf16[32,3072]{1,0:T(8,128)(2,1)} %copy-done.25, bf16[32,3072]{1,0:T(8,128)(2,1)} %copy-done.24, bf16[32,3072]{1,0:T(8,128)(2,1)} %copy-done.28, ...), custom_call_target="tpu_custom_call" | custom-call | tf_op jit(solution)/shard_map/pallas_call | solution.py:65
  196.8 4.0 %shard_map.88.refs_9_ = bf16[256,7168]{1,0:T(8,128)(2,1)} custom-call(bf16[256,512]{1,0:T(8,128)(2,1)} %convolution_convert_fusion.basis_ref, bf16[32,3072]{1,0:T(8,128)(2,1)} %copy-done.6, bf16[32,3072]{1,0:T(8,128)(2,1)} %copy-done.10, bf16[32,3072]{1,0:T(8,128)(2,1)} %copy-done.9, bf16[32,3072]{1,0:T(8,128)(2,1)} %copy-done.13, ...), custom_call_target="tpu_custom_call", output_to_operand_aliasing={{}: (18, {})} | custom-call | tf_op jit(solution)/shard_map/pallas_call | solution.py:65
  200.9 2.8 %shard_map.89 = bf16[256,7168]{1,0:T(8,128)(2,1)} custom-call(bf16[256,512]{1,0:T(8,128)(2,1)} %convolution_convert_fusion.basis_ref, bf16[64,1024]{1,0:T(8,128)(2,1)} %copy-done.8, bf16[64,1024]{1,0:T(8,128)(2,1)} %collective-permute-done.25.refs_1_, bf16[64,1024]{1,0:T(8,128)(2,1)} %collective-permute-done.26.refs_2_, ...), custom_call_target="tpu_custom_call", output_to_operand_aliasing={{}: (10, {})} | custom-call | tf_op jit(solution)/shard_map/pallas_call | solution.py:65
  (224 shorter events, 13.2 us)
Async XLA Ops:
  9.8 17.1 %collective-permute-start.2 = (bf16[128,2048]{1,0:T(8,128)(2,1)}, bf16[128,2048]{1,0:T(8,128)(2,1)S(1)}, u32[]{:S(2)}, u32[]{:S(2)}) collective-permute-start(bf16[128,2048]{1,0:T(8,128)(2,1)} %get-tuple-element.38), channel_id=1, source_target_pairs={{0,1},{1,0},{2,3},{3,2},{4,5},{5,4},{6,7},{7,6},{8,9},{9,8},{10,11... | collective-permute-start | bytes 1572872 | tf_op jit(solution)/shard_map/ppermute | solution.py:169
  23.7 26.2 %collective-permute-start.5 = (bf16[256,2048]{1,0:T(8,128)(2,1)}, bf16[256,2048]{1,0:T(8,128)(2,1)S(1)}, u32[]{:S(2)}, u32[]{:S(2)}) collective-permute-start(bf16[256,2048]{1,0:T(8,128)(2,1)} %get-tuple-element.43), channel_id=1, source_target_pairs={{0,1},{1,0},{2,3},{3,2},{4,5},{5,4},{6,7},{7,6},{8,9},{9,8},{10,11... | collective-permute-start | bytes 3145736 | tf_op jit(solution)/shard_map/ppermute | solution.py:169
  23.7 49.1 %collective-permute-start.1 = (bf16[128,2048]{1,0:T(8,128)(2,1)}, bf16[128,2048]{1,0:T(8,128)(2,1)}, u32[]{:S(2)}, u32[]{:S(2)}) collective-permute-start(bf16[128,2048]{1,0:T(8,128)(2,1)} %get-tuple-element.41), channel_id=1, source_target_pairs={{0,1},{1,0},{2,3},{3,2},{4,5},{5,4},{6,7},{7,6},{8,9},{9,8},{10,11... | collective-permute-start | bytes 1572872 | tf_op jit(solution)/shard_map/ppermute | solution.py:169
  26.7 63.1 %collective-permute-start = (bf16[256,512]{1,0:T(8,128)(2,1)S(1)}, bf16[256,512]{1,0:T(8,128)(2,1)}, u32[]{:S(2)}, u32[]{:S(2)}) collective-permute-start(bf16[256,512]{1,0:T(8,128)(2,1)S(1)} %constant_dynamic-slice_fusion), channel_id=1, source_target_pairs={{0,1},{1,0},{2,3},{3,2},{4,5},{5,4},{6,7},{7,6},{8,9},{9,8},{10,11... | collective-permute-start | bytes 786440 | tf_op jit(solution)/shard_map/ppermute | solution.py:210
  41.2 2.8 %collective-permute-start.3 = (bf16[64,7168]{1,0:T(8,128)(2,1)}, bf16[64,7168]{1,0:T(8,128)(2,1)}, u32[]{:S(2)}, u32[]{:S(2)}) collective-permute-start(bf16[64,7168]{1,0:T(8,128)(2,1)} %slice.299), channel_id=1, source_target_pairs={{0,2},{2,0},{4,6},{6,4},{8,10},{10,8},{12,14},{14,12},{16,18},{18,... | collective-permute-start | bytes 2752520 | tf_op jit(solution)/shard_map/ppermute | solution.py:165
  46.0 12.8 %collective-permute-start.4 = (bf16[32,7168]{1,0:T(8,128)(2,1)S(1)}, bf16[32,7168]{1,0:T(8,128)(2,1)S(1)}, u32[]{:S(2)}, u32[]{:S(2)}) collective-permute-start(bf16[32,7168]{1,0:T(8,128)(2,1)S(1)} %slice.304), channel_id=1, source_target_pairs={{0,4},{2,6},{4,0},{6,2},{8,12},{10,14},{12,8},{14,10},{16,20},{18,... | collective-permute-start | bytes 1376264 | tf_op jit(solution)/shard_map/ppermute | solution.py:165
  57.7 3.1 %collective-permute-start.7 = (bf16[128,3584]{1,0:T(8,128)(2,1)S(1)}, bf16[128,3584]{1,0:T(8,128)(2,1)S(1)}, u32[]{:S(2)}, u32[]{:S(2)}) collective-permute-start(bf16[128,3584]{1,0:T(8,128)(2,1)S(1)} %slice.298), channel_id=1, source_target_pairs={{0,2},{2,0},{4,6},{6,4},{8,10},{10,8},{12,14},{14,12},{16,18},{18,... | collective-permute-start | bytes 2752520 | tf_op jit(solution)/shard_map/ppermute | solution.py:165
  58.8 11.2 %collective-permute-start.6 = (bf16[16,7168]{1,0:T(8,128)(2,1)S(1)}, bf16[16,7168]{1,0:T(8,128)(2,1)S(1)}, u32[]{:S(2)}, u32[]{:S(2)}) collective-permute-start(bf16[16,7168]{1,0:T(8,128)(2,1)S(1)} %slice.309), channel_id=1, source_target_pairs={{0,8},{2,10},{4,12},{6,14},{8,0},{10,2},{12,4},{14,6},{16,24},{18,... | collective-permute-start | bytes 688136 | tf_op jit(solution)/shard_map/ppermute | solution.py:165
  61.0 27.2 %collective-permute-start.11 = (bf16[64,3584]{1,0:T(8,128)(2,1)S(1)}, bf16[64,3584]{1,0:T(8,128)(2,1)S(1)}, u32[]{:S(2)}, u32[]{:S(2)}) collective-permute-start(bf16[64,3584]{1,0:T(8,128)(2,1)S(1)} %slice.303), channel_id=1, source_target_pairs={{0,4},{2,6},{4,0},{6,2},{8,12},{10,14},{12,8},{14,10},{16,20},{18,... | collective-permute-start | bytes 1376264 | tf_op jit(solution)/shard_map/ppermute | solution.py:165
  70.0 10.7 %collective-permute-start.8 = (bf16[128,3584]{1,0:T(8,128)(2,1)S(1)}, bf16[128,3584]{1,0:T(8,128)(2,1)S(1)}, u32[]{:S(2)}, u32[]{:S(2)}) collective-permute-start(bf16[128,3584]{1,0:T(8,128)(2,1)S(1)} %slice.297), channel_id=1, source_target_pairs={{0,2},{2,0},{4,6},{6,4},{8,10},{10,8},{12,14},{14,12},{16,18},{18,... | collective-permute-start | bytes 2752520 | tf_op jit(solution)/shard_map/ppermute | solution.py:165
  70.1 22.6 %collective-permute-start.9 = (bf16[8,7168]{1,0:T(8,128)(2,1)S(1)}, bf16[8,7168]{1,0:T(8,128)(2,1)S(1)}, u32[]{:S(2)}, u32[]{:S(2)}) collective-permute-start(bf16[8,7168]{1,0:T(8,128)(2,1)S(1)} %slice.314), channel_id=1, source_target_pairs={{0,16},{2,18},{4,20},{6,22},{8,24},{10,26},{12,28},{14,30},{16,0},... | collective-permute-start | bytes 344072 | tf_op jit(solution)/shard_map/ppermute | solution.py:165
  80.4 7.5 %collective-permute-start.12 = (bf16[64,3584]{1,0:T(8,128)(2,1)S(1)}, bf16[64,3584]{1,0:T(8,128)(2,1)S(1)}, u32[]{:S(2)}, u32[]{:S(2)}) collective-permute-start(bf16[64,3584]{1,0:T(8,128)(2,1)S(1)} %slice.302), channel_id=1, source_target_pairs={{0,2},{2,0},{4,6},{6,4},{8,10},{10,8},{12,14},{14,12},{16,18},{18,... | collective-permute-start | bytes 1376264 | tf_op jit(solution)/shard_map/ppermute | solution.py:165
  80.9 13.5 %collective-permute-start.14 = (bf16[64,3584]{1,0:T(8,128)(2,1)S(1)}, bf16[64,3584]{1,0:T(8,128)(2,1)S(1)}, u32[]{:S(2)}, u32[]{:S(2)}) collective-permute-start(bf16[64,3584]{1,0:T(8,128)(2,1)S(1)} %slice.301), channel_id=1, source_target_pairs={{0,4},{2,6},{4,0},{6,2},{8,12},{10,14},{12,8},{14,10},{16,20},{18,... | collective-permute-start | bytes 1376264 | tf_op jit(solution)/shard_map/ppermute | solution.py:165
  87.9 4.1 %collective-permute-start.10 = (bf16[64,3584]{1,0:T(8,128)(2,1)S(1)}, bf16[64,3584]{1,0:T(8,128)(2,1)S(1)}, u32[]{:S(2)}, u32[]{:S(2)}) collective-permute-start(bf16[64,3584]{1,0:T(8,128)(2,1)S(1)} %slice.300), channel_id=1, source_target_pairs={{0,2},{2,0},{4,6},{6,4},{8,10},{10,8},{12,14},{14,12},{16,18},{18,... | collective-permute-start | bytes 1376264 | tf_op jit(solution)/shard_map/ppermute | solution.py:165
  88.2 11.2 %collective-permute-start.18 = (bf16[32,3584]{1,0:T(8,128)(2,1)S(1)}, bf16[32,3584]{1,0:T(8,128)(2,1)S(1)}, u32[]{:S(2)}, u32[]{:S(2)}) collective-permute-start(bf16[32,3584]{1,0:T(8,128)(2,1)S(1)} %slice.308), channel_id=1, source_target_pairs={{0,4},{2,6},{4,0},{6,2},{8,12},{10,14},{12,8},{14,10},{16,20},{18,... | collective-permute-start | bytes 688136 | tf_op jit(solution)/shard_map/ppermute | solution.py:165
  89.8 8.5 %collective-permute-start.13 = (bf16[32,3584]{1,0:T(8,128)(2,1)S(1)}, bf16[32,3584]{1,0:T(8,128)(2,1)S(1)}, u32[]{:S(2)}, u32[]{:S(2)}) collective-permute-start(bf16[32,3584]{1,0:T(8,128)(2,1)S(1)} %slice.307), channel_id=1, source_target_pairs={{0,8},{2,10},{4,12},{6,14},{8,0},{10,2},{12,4},{14,6},{16,24},{18,... | collective-permute-start | bytes 688136 | tf_op jit(solution)/shard_map/ppermute | solution.py:165
  92.1 11.4 %collective-permute-start.17 = (bf16[32,3584]{1,0:T(8,128)(2,1)S(1)}, bf16[32,3584]{1,0:T(8,128)(2,1)S(1)}, u32[]{:S(2)}, u32[]{:S(2)}) collective-permute-start(bf16[32,3584]{1,0:T(8,128)(2,1)S(1)} %slice.306), channel_id=1, source_target_pairs={{0,4},{2,6},{4,0},{6,2},{8,12},{10,14},{12,8},{14,10},{16,20},{18,... | collective-permute-start | bytes 688136 | tf_op jit(solution)/shard_map/ppermute | solution.py:165
  94.5 11.0 %collective-permute-start.16 = (bf16[32,3584]{1,0:T(8,128)(2,1)S(1)}, bf16[32,3584]{1,0:T(8,128)(2,1)S(1)}, u32[]{:S(2)}, u32[]{:S(2)}) collective-permute-start(bf16[32,3584]{1,0:T(8,128)(2,1)S(1)} %slice.305), channel_id=1, source_target_pairs={{0,8},{2,10},{4,12},{6,14},{8,0},{10,2},{12,4},{14,6},{16,24},{18,... | collective-permute-start | bytes 688136 | tf_op jit(solution)/shard_map/ppermute | solution.py:165
  98.4 7.5 %collective-permute-start.15 = (bf16[16,3584]{1,0:T(8,128)(2,1)S(1)}, bf16[16,3584]{1,0:T(8,128)(2,1)S(1)}, u32[]{:S(2)}, u32[]{:S(2)}) collective-permute-start(bf16[16,3584]{1,0:T(8,128)(2,1)S(1)} %slice.313), channel_id=1, source_target_pairs={{0,16},{2,18},{4,20},{6,22},{8,24},{10,26},{12,28},{14,30},{16,0},... | collective-permute-start | bytes 344072 | tf_op jit(solution)/shard_map/ppermute | solution.py:165
  99.5 9.9 %collective-permute-start.21 = (bf16[16,3584]{1,0:T(8,128)(2,1)S(1)}, bf16[16,3584]{1,0:T(8,128)(2,1)S(1)}, u32[]{:S(2)}, u32[]{:S(2)}) collective-permute-start(bf16[16,3584]{1,0:T(8,128)(2,1)S(1)} %slice.312), channel_id=1, source_target_pairs={{0,8},{2,10},{4,12},{6,14},{8,0},{10,2},{12,4},{14,6},{16,24},{18,... | collective-permute-start | bytes 344072 | tf_op jit(solution)/shard_map/ppermute | solution.py:165
  103.6 8.1 %collective-permute-start.20 = (bf16[16,3584]{1,0:T(8,128)(2,1)S(1)}, bf16[16,3584]{1,0:T(8,128)(2,1)S(1)}, u32[]{:S(2)}, u32[]{:S(2)}) collective-permute-start(bf16[16,3584]{1,0:T(8,128)(2,1)S(1)} %slice.311), channel_id=1, source_target_pairs={{0,8},{2,10},{4,12},{6,14},{8,0},{10,2},{12,4},{14,6},{16,24},{18,... | collective-permute-start | bytes 344072 | tf_op jit(solution)/shard_map/ppermute | solution.py:165
  105.6 11.3 %collective-permute-start.19 = (bf16[16,3584]{1,0:T(8,128)(2,1)S(1)}, bf16[16,3584]{1,0:T(8,128)(2,1)S(1)}, u32[]{:S(2)}, u32[]{:S(2)}) collective-permute-start(bf16[16,3584]{1,0:T(8,128)(2,1)S(1)} %slice.310), channel_id=1, source_target_pairs={{0,16},{2,18},{4,20},{6,22},{8,24},{10,26},{12,28},{14,30},{16,0},... | collective-permute-start | bytes 344072 | tf_op jit(solution)/shard_map/ppermute | solution.py:165
  109.5 8.1 %collective-permute-start.22 = (bf16[8,3584]{1,0:T(8,128)(2,1)S(1)}, bf16[8,3584]{1,0:T(8,128)(2,1)S(1)}, u32[]{:S(2)}, u32[]{:S(2)}) collective-permute-start(bf16[8,3584]{1,0:T(8,128)(2,1)S(1)} %slice.316), channel_id=1, source_target_pairs={{0,16},{2,18},{4,20},{6,22},{8,24},{10,26},{12,28},{14,30},{16,0},... | collective-permute-start | bytes 172040 | tf_op jit(solution)/shard_map/ppermute | solution.py:165
  111.7 6.5 %collective-permute-start.23 = (bf16[8,3584]{1,0:T(8,128)(2,1)S(1)}, bf16[8,3584]{1,0:T(8,128)(2,1)S(1)}, u32[]{:S(2)}, u32[]{:S(2)}) collective-permute-start(bf16[8,3584]{1,0:T(8,128)(2,1)S(1)} %slice.315), channel_id=1, source_target_pairs={{0,16},{2,18},{4,20},{6,22},{8,24},{10,26},{12,28},{14,30},{16,0},... | collective-permute-start | bytes 172040 | tf_op jit(solution)/shard_map/ppermute | solution.py:165
  133.8 58.1 %copy-start.7 = (bf16[32,3072]{1,0:T(8,128)(2,1)}, bf16[32,3072]{1,0:T(8,128)(2,1)S(1)}, u32[]{:S(2)}) copy-start(bf16[32,3072]{1,0:T(8,128)(2,1)S(1)} %get-tuple-element.76.refs_0_) | copy-start | bytes 589828
  133.8 62.2 %copy-start.6 = (bf16[32,3072]{1,0:T(8,128)(2,1)}, bf16[32,3072]{1,0:T(8,128)(2,1)S(1)}, u32[]{:S(2)}) copy-start(bf16[32,3072]{1,0:T(8,128)(2,1)S(1)} %get-tuple-element.77.refs_0_) | copy-start | bytes 589828
  133.8 9.2 %collective-permute-start.48 = (bf16[32,3072]{1,0:T(8,128)(2,1)S(1)}, bf16[32,3072]{1,0:T(8,128)(2,1)S(1)}, u32[]{:S(2)}, u32[]{:S(2)}) collective-permute-start(bf16[32,3072]{1,0:T(8,128)(2,1)S(1)} %get-tuple-element.76.refs_0_), channel_id=1, source_target_pairs={{0,8},{2,10},{4,12},{6,14},{8,16},{10,18},{12,20},{14,22},{16,24},... | collective-permute-start | bytes 589832 | tf_op jit(solution)/shard_map/ppermute | solution.py:303
  133.9 9.3 %collective-permute-start.47 = (bf16[32,3072]{1,0:T(8,128)(2,1)S(1)}, bf16[32,3072]{1,0:T(8,128)(2,1)S(1)}, u32[]{:S(2)}, u32[]{:S(2)}) collective-permute-start(bf16[32,3072]{1,0:T(8,128)(2,1)S(1)} %get-tuple-element.76.refs_0_), channel_id=1, source_target_pairs={{0,4},{2,6},{4,0},{6,2},{8,12},{10,14},{12,8},{14,10},{16,20},{18,... | collective-permute-start | bytes 589832 | tf_op jit(solution)/shard_map/ppermute | solution.py:165
  134.6 7.4 %collective-permute-start.24 = (bf16[32,1024]{1,0:T(8,128)(2,1)S(1)}, bf16[32,1024]{1,0:T(8,128)(2,1)S(1)}, u32[]{:S(2)}, u32[]{:S(2)}) collective-permute-start(bf16[32,1024]{1,0:T(8,128)(2,1)S(1)} %slice.246), channel_id=1, source_target_pairs={{0,4},{2,6},{4,0},{6,2},{8,12},{10,14},{12,8},{14,10},{16,20},{18,... | collective-permute-start | bytes 196616 | tf_op jit(solution)/shard_map/ppermute | solution.py:165
  136.0 7.2 %collective-permute-start.54 = (bf16[32,3072]{1,0:T(8,128)(2,1)S(1)}, bf16[32,3072]{1,0:T(8,128)(2,1)S(1)}, u32[]{:S(2)}, u32[]{:S(2)}) collective-permute-start(bf16[32,3072]{1,0:T(8,128)(2,1)S(1)} %get-tuple-element.76.refs_0_), channel_id=1, source_target_pairs={{0,2},{2,0},{4,6},{6,4},{8,10},{10,8},{12,14},{14,12},{16,18},{18,... | collective-permute-start | bytes 589832 | tf_op jit(solution)/shard_map/ppermute | solution.py:165
  136.0 15.3 %collective-permute-start.33 = (bf16[32,3072]{1,0:T(8,128)(2,1)S(1)}, bf16[32,3072]{1,0:T(8,128)(2,1)S(1)}, u32[]{:S(2)}, u32[]{:S(2)}) collective-permute-start(bf16[32,3072]{1,0:T(8,128)(2,1)S(1)} %get-tuple-element.77.refs_0_), channel_id=1, source_target_pairs={{0,8},{2,10},{4,12},{6,14},{8,16},{10,18},{12,20},{14,22},{16,24},... | collective-permute-start | bytes 589832 | tf_op jit(solution)/shard_map/ppermute | solution.py:303
  142.0 10.2 %collective-permute-start.32 = (bf16[32,3072]{1,0:T(8,128)(2,1)S(1)}, bf16[32,3072]{1,0:T(8,128)(2,1)S(1)}, u32[]{:S(2)}, u32[]{:S(2)}) collective-permute-start(bf16[32,3072]{1,0:T(8,128)(2,1)S(1)} %get-tuple-element.77.refs_0_), channel_id=1, source_target_pairs={{0,4},{2,6},{4,0},{6,2},{8,12},{10,14},{12,8},{14,10},{16,20},{18,... | collective-permute-start | bytes 589832 | tf_op jit(solution)/shard_map/ppermute | solution.py:165
  143.0 8.3 %collective-permute-start.25 = (bf16[64,1024]{1,0:T(8,128)(2,1)S(1)}, bf16[64,1024]{1,0:T(8,128)(2,1)}, u32[]{:S(2)}, u32[]{:S(2)}) collective-permute-start(bf16[64,1024]{1,0:T(8,128)(2,1)S(1)} %pad_maximum_fusion.refs_0_), channel_id=1, source_target_pairs={{0,8},{2,10},{4,12},{6,14},{8,16},{10,18},{12,20},{14,22},{16,24},... | collective-permute-start | bytes 393224 | tf_op jit(solution)/shard_map/ppermute | solution.py:299
  143.2 9.0 %collective-permute-start.39 = (bf16[32,3072]{1,0:T(8,128)(2,1)S(1)}, bf16[32,3072]{1,0:T(8,128)(2,1)S(1)}, u32[]{:S(2)}, u32[]{:S(2)}) collective-permute-start(bf16[32,3072]{1,0:T(8,128)(2,1)S(1)} %get-tuple-element.77.refs_0_), channel_id=1, source_target_pairs={{0,2},{2,0},{4,6},{6,4},{8,10},{10,8},{12,14},{14,12},{16,18},{18,... | collective-permute-start | bytes 589832 | tf_op jit(solution)/shard_map/ppermute | solution.py:165
  143.2 15.1 %collective-permute-start.50 = (bf16[32,3072]{1,0:T(8,128)(2,1)S(1)}, bf16[32,3072]{1,0:T(8,128)(2,1)S(1)}, u32[]{:S(2)}, u32[]{:S(2)}) collective-permute-start(bf16[32,3072]{1,0:T(8,128)(2,1)S(1)} %collective-permute-done.48.refs_2_), channel_id=1, source_target_pairs={{0,8},{2,10},{4,12},{6,14},{8,16},{10,18},{12,20},{14,22},{16,24},... | collective-permute-start | bytes 589832 | tf_op jit(solution)/shard_map/ppermute | solution.py:303
  151.2 7.1 %collective-permute-start.26 = (bf16[64,1024]{1,0:T(8,128)(2,1)}, bf16[64,1024]{1,0:T(8,128)(2,1)}, u32[]{:S(2)}, u32[]{:S(2)}) collective-permute-start(bf16[64,1024]{1,0:T(8,128)(2,1)} %collective-permute-done.25.refs_1_), channel_id=1, source_target_pairs={{0,8},{2,10},{4,12},{6,14},{8,16},{10,18},{12,20},{14,22},{16,24},... | collective-permute-start | bytes 393224 | tf_op jit(solution)/shard_map/ppermute | solution.py:299
  151.2 8.0 %collective-permute-start.49 = (bf16[32,3072]{1,0:T(8,128)(2,1)S(1)}, bf16[32,3072]{1,0:T(8,128)(2,1)S(1)}, u32[]{:S(2)}, u32[]{:S(2)}) collective-permute-start(bf16[32,3072]{1,0:T(8,128)(2,1)S(1)} %collective-permute-done.48.refs_2_), channel_id=1, source_target_pairs={{0,4},{2,6},{4,0},{6,2},{8,12},{10,14},{12,8},{14,10},{16,20},{18,... | collective-permute-start | bytes 589832 | tf_op jit(solution)/shard_map/ppermute | solution.py:165
  152.2 7.1 %collective-permute-start.55 = (bf16[32,3072]{1,0:T(8,128)(2,1)S(1)}, bf16[32,3072]{1,0:T(8,128)(2,1)S(1)}, u32[]{:S(2)}, u32[]{:S(2)}) collective-permute-start(bf16[32,3072]{1,0:T(8,128)(2,1)S(1)} %collective-permute-done.47.refs_1_), channel_id=1, source_target_pairs={{0,2},{2,0},{4,6},{6,4},{8,10},{10,8},{12,14},{14,12},{16,18},{18,... | collective-permute-start | bytes 589832 | tf_op jit(solution)/shard_map/ppermute | solution.py:165
  152.2 7.6 %collective-permute-start.56 = (bf16[32,3072]{1,0:T(8,128)(2,1)S(1)}, bf16[32,3072]{1,0:T(8,128)(2,1)S(1)}, u32[]{:S(2)}, u32[]{:S(2)}) collective-permute-start(bf16[32,3072]{1,0:T(8,128)(2,1)S(1)} %collective-permute-done.48.refs_2_), channel_id=1, source_target_pairs={{0,2},{2,0},{4,6},{6,4},{8,10},{10,8},{12,14},{14,12},{16,18},{18,... | collective-permute-start | bytes 589832 | tf_op jit(solution)/shard_map/ppermute | solution.py:165
  158.3 8.5 %collective-permute-start.35 = (bf16[32,3072]{1,0:T(8,128)(2,1)S(1)}, bf16[32,3072]{1,0:T(8,128)(2,1)S(1)}, u32[]{:S(2)}, u32[]{:S(2)}) collective-permute-start(bf16[32,3072]{1,0:T(8,128)(2,1)S(1)} %collective-permute-done.33.refs_2_), channel_id=1, source_target_pairs={{0,8},{2,10},{4,12},{6,14},{8,16},{10,18},{12,20},{14,22},{16,24},... | collective-permute-start | bytes 589832 | tf_op jit(solution)/shard_map/ppermute | solution.py:303
  158.3 8.5 %collective-permute-start.34 = (bf16[32,3072]{1,0:T(8,128)(2,1)S(1)}, bf16[32,3072]{1,0:T(8,128)(2,1)S(1)}, u32[]{:S(2)}, u32[]{:S(2)}) collective-permute-start(bf16[32,3072]{1,0:T(8,128)(2,1)S(1)} %collective-permute-done.33.refs_2_), channel_id=1, source_target_pairs={{0,4},{2,6},{4,0},{6,2},{8,12},{10,14},{12,8},{14,10},{16,20},{18,... | collective-permute-start | bytes 589832 | tf_op jit(solution)/shard_map/ppermute | solution.py:165
  159.3 8.3 %collective-permute-start.40 = (bf16[32,3072]{1,0:T(8,128)(2,1)S(1)}, bf16[32,3072]{1,0:T(8,128)(2,1)S(1)}, u32[]{:S(2)}, u32[]{:S(2)}) collective-permute-start(bf16[32,3072]{1,0:T(8,128)(2,1)S(1)} %collective-permute-done.32.refs_1_), channel_id=1, source_target_pairs={{0,2},{2,0},{4,6},{6,4},{8,10},{10,8},{12,14},{14,12},{16,18},{18,... | collective-permute-start | bytes 589832 | tf_op jit(solution)/shard_map/ppermute | solution.py:165
  159.3 8.3 %collective-permute-start.41 = (bf16[32,3072]{1,0:T(8,128)(2,1)S(1)}, bf16[32,3072]{1,0:T(8,128)(2,1)S(1)}, u32[]{:S(2)}, u32[]{:S(2)}) collective-permute-start(bf16[32,3072]{1,0:T(8,128)(2,1)S(1)} %collective-permute-done.33.refs_2_), channel_id=1, source_target_pairs={{0,2},{2,0},{4,6},{6,4},{8,10},{10,8},{12,14},{14,12},{16,18},{18,... | collective-permute-start | bytes 589832 | tf_op jit(solution)/shard_map/ppermute | solution.py:165
  159.8 10.0 %collective-permute-start.27 = (bf16[64,1024]{1,0:T(8,128)(2,1)}, bf16[64,1024]{1,0:T(8,128)(2,1)}, u32[]{:S(2)}, u32[]{:S(2)}) collective-permute-start(bf16[64,1024]{1,0:T(8,128)(2,1)} %collective-permute-done.26.refs_2_), channel_id=1, source_target_pairs={{0,8},{2,10},{4,12},{6,14},{8,16},{10,18},{12,20},{14,22},{16,24},... | collective-permute-start | bytes 393224 | tf_op jit(solution)/shard_map/ppermute | solution.py:299
  166.9 9.0 %collective-permute-start.52 = (bf16[32,3072]{1,0:T(8,128)(2,1)S(1)}, bf16[32,3072]{1,0:T(8,128)(2,1)S(1)}, u32[]{:S(2)}, u32[]{:S(2)}) collective-permute-start(bf16[32,3072]{1,0:T(8,128)(2,1)S(1)} %collective-permute-done.50.refs_4_), channel_id=1, source_target_pairs={{0,8},{2,10},{4,12},{6,14},{8,16},{10,18},{12,20},{14,22},{16,24},... | collective-permute-start | bytes 589832 | tf_op jit(solution)/shard_map/ppermute | solution.py:303
  166.9 9.0 %collective-permute-start.51 = (bf16[32,3072]{1,0:T(8,128)(2,1)S(1)}, bf16[32,3072]{1,0:T(8,128)(2,1)S(1)}, u32[]{:S(2)}, u32[]{:S(2)}) collective-permute-start(bf16[32,3072]{1,0:T(8,128)(2,1)S(1)} %collective-permute-done.50.refs_4_), channel_id=1, source_target_pairs={{0,4},{2,6},{4,0},{6,2},{8,12},{10,14},{12,8},{14,10},{16,20},{18,... | collective-permute-start | bytes 589832 | tf_op jit(solution)/shard_map/ppermute | solution.py:165
  167.6 8.4 %collective-permute-start.57 = (bf16[32,3072]{1,0:T(8,128)(2,1)S(1)}, bf16[32,3072]{1,0:T(8,128)(2,1)S(1)}, u32[]{:S(2)}, u32[]{:S(2)}) collective-permute-start(bf16[32,3072]{1,0:T(8,128)(2,1)S(1)} %collective-permute-done.49.refs_3_), channel_id=1, source_target_pairs={{0,2},{2,0},{4,6},{6,4},{8,10},{10,8},{12,14},{14,12},{16,18},{18,... | collective-permute-start | bytes 589832 | tf_op jit(solution)/shard_map/ppermute | solution.py:165
  167.6 8.9 %collective-permute-start.58 = (bf16[32,3072]{1,0:T(8,128)(2,1)S(1)}, bf16[32,3072]{1,0:T(8,128)(2,1)S(1)}, u32[]{:S(2)}, u32[]{:S(2)}) collective-permute-start(bf16[32,3072]{1,0:T(8,128)(2,1)S(1)} %collective-permute-done.50.refs_4_), channel_id=1, source_target_pairs={{0,2},{2,0},{4,6},{6,4},{8,10},{10,8},{12,14},{14,12},{16,18},{18,... | collective-permute-start | bytes 589832 | tf_op jit(solution)/shard_map/ppermute | solution.py:165
  169.8 8.8 %collective-permute-start.37 = (bf16[32,3072]{1,0:T(8,128)(2,1)S(1)}, bf16[32,3072]{1,0:T(8,128)(2,1)S(1)}, u32[]{:S(2)}, u32[]{:S(2)}) collective-permute-start(bf16[32,3072]{1,0:T(8,128)(2,1)S(1)} %collective-permute-done.35.refs_4_), channel_id=1, source_target_pairs={{0,8},{2,10},{4,12},{6,14},{8,16},{10,18},{12,20},{14,22},{16,24},... | collective-permute-start | bytes 589832 | tf_op jit(solution)/shard_map/ppermute | solution.py:303
  175.9 7.8 %collective-permute-start.36 = (bf16[32,3072]{1,0:T(8,128)(2,1)S(1)}, bf16[32,3072]{1,0:T(8,128)(2,1)S(1)}, u32[]{:S(2)}, u32[]{:S(2)}) collective-permute-start(bf16[32,3072]{1,0:T(8,128)(2,1)S(1)} %collective-permute-done.35.refs_4_), channel_id=1, source_target_pairs={{0,4},{2,6},{4,0},{6,2},{8,12},{10,14},{12,8},{14,10},{16,20},{18,... | collective-permute-start | bytes 589832 | tf_op jit(solution)/shard_map/ppermute | solution.py:165
  175.9 7.8 %collective-permute-start.42 = (bf16[32,3072]{1,0:T(8,128)(2,1)S(1)}, bf16[32,3072]{1,0:T(8,128)(2,1)S(1)}, u32[]{:S(2)}, u32[]{:S(2)}) collective-permute-start(bf16[32,3072]{1,0:T(8,128)(2,1)S(1)} %collective-permute-done.34.refs_3_), channel_id=1, source_target_pairs={{0,2},{2,0},{4,6},{6,4},{8,10},{10,8},{12,14},{14,12},{16,18},{18,... | collective-permute-start | bytes 589832 | tf_op jit(solution)/shard_map/ppermute | solution.py:165
  176.0 7.8 %collective-permute-start.43 = (bf16[32,3072]{1,0:T(8,128)(2,1)S(1)}, bf16[32,3072]{1,0:T(8,128)(2,1)S(1)}, u32[]{:S(2)}, u32[]{:S(2)}) collective-permute-start(bf16[32,3072]{1,0:T(8,128)(2,1)S(1)} %collective-permute-done.35.refs_4_), channel_id=1, source_target_pairs={{0,2},{2,0},{4,6},{6,4},{8,10},{10,8},{12,14},{14,12},{16,18},{18,... | collective-permute-start | bytes 589832 | tf_op jit(solution)/shard_map/ppermute | solution.py:165
  176.5 11.3 %collective-permute-start.53 = (bf16[32,3072]{1,0:T(8,128)(2,1)S(1)}, bf16[32,3072]{1,0:T(8,128)(2,1)S(1)}, u32[]{:S(2)}, u32[]{:S(2)}) collective-permute-start(bf16[32,3072]{1,0:T(8,128)(2,1)S(1)} %collective-permute-done.52.refs_6_), channel_id=1, source_target_pairs={{0,4},{2,6},{4,0},{6,2},{8,12},{10,14},{12,8},{14,10},{16,20},{18,... | collective-permute-start | bytes 589832 | tf_op jit(solution)/shard_map/ppermute | solution.py:165
  178.6 9.3 %collective-permute-start.59 = (bf16[32,3072]{1,0:T(8,128)(2,1)S(1)}, bf16[32,3072]{1,0:T(8,128)(2,1)S(1)}, u32[]{:S(2)}, u32[]{:S(2)}) collective-permute-start(bf16[32,3072]{1,0:T(8,128)(2,1)S(1)} %collective-permute-done.51.refs_5_), channel_id=1, source_target_pairs={{0,2},{2,0},{4,6},{6,4},{8,10},{10,8},{12,14},{14,12},{16,18},{18,... | collective-permute-start | bytes 589832 | tf_op jit(solution)/shard_map/ppermute | solution.py:165
  183.7 6.3 %collective-permute-start.38 = (bf16[32,3072]{1,0:T(8,128)(2,1)S(1)}, bf16[32,3072]{1,0:T(8,128)(2,1)S(1)}, u32[]{:S(2)}, u32[]{:S(2)}) collective-permute-start(bf16[32,3072]{1,0:T(8,128)(2,1)S(1)} %collective-permute-done.37.refs_6_), channel_id=1, source_target_pairs={{0,4},{2,6},{4,0},{6,2},{8,12},{10,14},{12,8},{14,10},{16,20},{18,... | collective-permute-start | bytes 589832 | tf_op jit(solution)/shard_map/ppermute | solution.py:165
  183.7 6.2 %collective-permute-start.60 = (bf16[32,3072]{1,0:T(8,128)(2,1)S(1)}, bf16[32,3072]{1,0:T(8,128)(2,1)S(1)}, u32[]{:S(2)}, u32[]{:S(2)}) collective-permute-start(bf16[32,3072]{1,0:T(8,128)(2,1)S(1)} %collective-permute-done.52.refs_6_), channel_id=1, source_target_pairs={{0,2},{2,0},{4,6},{6,4},{8,10},{10,8},{12,14},{14,12},{16,18},{18,... | collective-permute-start | bytes 589832 | tf_op jit(solution)/shard_map/ppermute | solution.py:165
  183.8 6.7 %collective-permute-start.44 = (bf16[32,3072]{1,0:T(8,128)(2,1)S(1)}, bf16[32,3072]{1,0:T(8,128)(2,1)S(1)}, u32[]{:S(2)}, u32[]{:S(2)}) collective-permute-start(bf16[32,3072]{1,0:T(8,128)(2,1)S(1)} %collective-permute-done.36.refs_5_), channel_id=1, source_target_pairs={{0,2},{2,0},{4,6},{6,4},{8,10},{10,8},{12,14},{14,12},{16,18},{18,... | collective-permute-start | bytes 589832 | tf_op jit(solution)/shard_map/ppermute | solution.py:165
  187.8 2.7 %collective-permute-start.45 = (bf16[32,3072]{1,0:T(8,128)(2,1)S(1)}, bf16[32,3072]{1,0:T(8,128)(2,1)S(1)}, u32[]{:S(2)}, u32[]{:S(2)}) collective-permute-start(bf16[32,3072]{1,0:T(8,128)(2,1)S(1)} %collective-permute-done.37.refs_6_), channel_id=1, source_target_pairs={{0,2},{2,0},{4,6},{6,4},{8,10},{10,8},{12,14},{14,12},{16,18},{18,... | collective-permute-start | bytes 589832 | tf_op jit(solution)/shard_map/ppermute | solution.py:165
  187.8 3.2 %collective-permute-start.61 = (bf16[32,3072]{1,0:T(8,128)(2,1)S(1)}, bf16[32,3072]{1,0:T(8,128)(2,1)S(1)}, u32[]{:S(2)}, u32[]{:S(2)}) collective-permute-start(bf16[32,3072]{1,0:T(8,128)(2,1)S(1)} %collective-permute-done.53.refs_7_), channel_id=1, source_target_pairs={{0,2},{2,0},{4,6},{6,4},{8,10},{10,8},{12,14},{14,12},{16,18},{18,... | collective-permute-start | bytes 589832 | tf_op jit(solution)/shard_map/ppermute | solution.py:165
  189.9 6.2 %collective-permute-start.46 = (bf16[32,3072]{1,0:T(8,128)(2,1)S(1)}, bf16[32,3072]{1,0:T(8,128)(2,1)S(1)}, u32[]{:S(2)}, u32[]{:S(2)}) collective-permute-start(bf16[32,3072]{1,0:T(8,128)(2,1)S(1)} %collective-permute-done.38.refs_7_), channel_id=1, source_target_pairs={{0,2},{2,0},{4,6},{6,4},{8,10},{10,8},{12,14},{14,12},{16,18},{18,... | collective-permute-start | bytes 589832 | tf_op jit(solution)/shard_map/ppermute | solution.py:165
  189.9 10.9 %collective-permute-start.28 = (bf16[64,1024]{1,0:T(8,128)(2,1)S(1)}, bf16[64,1024]{1,0:T(8,128)(2,1)}, u32[]{:S(2)}, u32[]{:S(2)}) collective-permute-start(bf16[64,1024]{1,0:T(8,128)(2,1)S(1)} %pad_maximum_fusion.refs_0_), channel_id=1, source_target_pairs={{0,2},{2,0},{4,6},{6,4},{8,10},{10,8},{12,14},{14,12},{16,18},{18,... | collective-permute-start | bytes 393224 | tf_op jit(solution)/shard_map/ppermute | solution.py:165
  190.5 10.4 %collective-permute-start.29 = (bf16[64,1024]{1,0:T(8,128)(2,1)}, bf16[64,1024]{1,0:T(8,128)(2,1)}, u32[]{:S(2)}, u32[]{:S(2)}) collective-permute-start(bf16[64,1024]{1,0:T(8,128)(2,1)} %collective-permute-done.25.refs_1_), channel_id=1, source_target_pairs={{0,2},{2,0},{4,6},{6,4},{8,10},{10,8},{12,14},{14,12},{16,18},{18,... | collective-permute-start | bytes 393224 | tf_op jit(solution)/shard_map/ppermute | solution.py:165
  190.5 10.3 %collective-permute-start.30 = (bf16[64,1024]{1,0:T(8,128)(2,1)}, bf16[64,1024]{1,0:T(8,128)(2,1)}, u32[]{:S(2)}, u32[]{:S(2)}) collective-permute-start(bf16[64,1024]{1,0:T(8,128)(2,1)} %collective-permute-done.26.refs_2_), channel_id=1, source_target_pairs={{0,2},{2,0},{4,6},{6,4},{8,10},{10,8},{12,14},{14,12},{16,18},{18,... | collective-permute-start | bytes 393224 | tf_op jit(solution)/shard_map/ppermute | solution.py:165
  191.8 9.0 %collective-permute-start.31 = (bf16[64,1024]{1,0:T(8,128)(2,1)}, bf16[64,1024]{1,0:T(8,128)(2,1)}, u32[]{:S(2)}, u32[]{:S(2)}) collective-permute-start(bf16[64,1024]{1,0:T(8,128)(2,1)} %collective-permute-done.27.refs_3_), channel_id=1, source_target_pairs={{0,2},{2,0},{4,6},{6,4},{8,10},{10,8},{12,14},{14,12},{16,18},{18,... | collective-permute-start | bytes 393224 | tf_op jit(solution)/shard_map/ppermute | solution.py:165
  (37 other events, 804.9 us)
where the time goes:
time: 204 us
  waiting for transfers between devices  67.5 us (33%)
  matrix products  39.9 us (20%)
  starting transfers between devices  37 us (18%)
  Pallas kernels  28.7 us (14%)
  blocking collectives  10.9 us (5%)
  other arithmetic  9.37 us (5%)
  local copies, waits for them, and re-layouts  7.83 us (4%)
  between operations  2.37 us (1%)
    dot_general x5, matrix products, gradient_part(): jnp.dot(projected, grad_out[:, start:start + width], preferred_element_ty...  38.8 us
    ppermute x49, waiting for transfers between devices, hop(): return lax.ppermute(value, 'dp', pairs[stage])  38.1 us
    ppermute x49, starting transfers between devices, hop(): return lax.ppermute(value, 'dp', pairs[stage])  29.4 us
    pallas_call x2, Pallas kernels, projections(): pl.pallas_call(functools.partial(projection_kernel, counts), grid=(tokens...  17.9 us
    ppermute x3, waiting for transfers between devices, body(): blocks.append(lax.ppermute(blocks[-1], 'dp', ring))  13.9 us
    ppermute x6, waiting for transfers between devices, body(): mine = lax.ppermute(mine, 'dp', ring)  13.5 us
    all_to_all x1, blocking collectives, body(): lax.all_to_all(everywhere, ('dp', 'shard'), 0, 0, tiled=True).sum(0)  10.9 us
    pallas_call x3, Pallas kernels, last_product(): pl.pallas_call(functools.partial(last_kernel, len(parts)), grid=(width //...  10.8 us
  transfers between devices with their start and end apart: 62, of which 24 were waited for; matrix products, arithmetic and copies ran while one was open for 24% of the time, Pallas kernels for 9%

commit v1 on v0

--- a/solution.py
+++ b/solution.py
@@ -10,7 +10,7 @@
 
 first_fix = 0.9999734386011124
 second_fix = 0.994079470779666
-PROJECTION_TILE = 512
+PROJECTION_TILE = 1024
 LAST_UNITS = 14
 RANK_PARTS = (1, 2, 1)
 COLUMN_PARTS = (1, 2, 2)
@@ -266,15 +266,14 @@
         rows.append(jnp.concatenate([d for d, u in zip(done, units) if u[0] == chunk], axis=1))
     gradient = jnp.concatenate(rows, axis=0)
 
-    squares = jnp.sum(gradient * gradient).reshape(1, 1)
-    squares = jnp.broadcast_to(squares, (8, 128))
+    squares = (gradient * gradient).reshape(own_rows // 8, 8, columns // 128, 128).sum((0, 2))
     devices = dp * shard
     if shard == 2:
         everywhere = jnp.broadcast_to(squares[None], (devices, 8, 128))
         squares = lax.all_to_all(everywhere, ("dp", "shard"), 0, 0, tiled=True).sum(0)
     else:
         squares = lax.psum(squares, ("dp", "shard"))
-    square_sum = squares[0, 0]
+    square_sum = jnp.sum(squares)
     whole = rank * columns * shard
     root_mean = jnp.sqrt(square_sum / whole + 1e-06)
     clip_factor = jnp.minimum(1.0, 4.0 / root_mean)

time: 204 us -> 202 us (level)
  no operation moved by 1% of the time
where the time goes in v1:
time: 202 us; the launch traced here: 201 us
  waiting for transfers between devices  67.6 us (33%)
  matrix products  40.1 us (20%)
  starting transfers between devices  36.9 us (18%)
  Pallas kernels  27.6 us (14%)
  blocking collectives  10.9 us (5%)
  other arithmetic  9.37 us (5%)
  local copies, waits for them, and re-layouts  6.68 us (3%)
  between operations  2.37 us (1%)
    dot_general x5, matrix products, gradient_part(): jnp.dot(projected, grad_out[:, start:start + width], preferred_element_ty...  39 us
    ppermute x49, waiting for transfers between devices, hop(): return lax.ppermute(value, 'dp', pairs[stage])  38.2 us
    ppermute x49, starting transfers between devices, hop(): return lax.ppermute(value, 'dp', pairs[stage])  29.3 us
    pallas_call x2, Pallas kernels, projections(): pl.pallas_call(functools.partial(projection_kernel, counts), grid=(tokens...  16.7 us
    ppermute x3, waiting for transfers between devices, body(): blocks.append(lax.ppermute(blocks[-1], 'dp', ring))  13.9 us
    ppermute x6, waiting for transfers between devices, body(): mine = lax.ppermute(mine, 'dp', ring)  13.5 us
    all_to_all x1, blocking collectives, body(): lax.all_to_all(everywhere, ('dp', 'shard'), 0, 0, tiled=True).sum(0)  10.9 us
    pallas_call x3, Pallas kernels, last_product(): pl.pallas_call(functools.partial(last_kernel, len(parts)), grid=(width //...  10.8 us
  transfers between devices with their start and end apart: 62, of which 24 were waited for; matrix products, arithmetic and copies ran while one was open for 24% of the time, Pallas kernels for 9%

profile of v1, /device:TPU:0, one launch (start us, length us, event | category | flops | bytes accessed | tf_op | source)
XLA Modules:
  0.0 201.5 jit_solution(14242198949585003214)
XLA Ops:
  0.8 0.8 fusion.13.pick_ref
  1.6 7.6 %shard_map.85 = (f32[128,2048]{1,0:T(8,128)}, bf16[128,2048]{1,0:T(8,128)(2,1)}) custom-call(bf16[128,512]{1,0:T(8,128)(2,1)} %fusion.13.pick_ref, bf16[2048,512]{1,0:T(8,128)(2,1)} %projector_ref.3, bf16[2048,2048]{1,0:T(8,128)(2,1)} %acts_ref.3), custom_call_target="tpu_custom_call" | custom-call | tf_op jit(solution)/shard_map/pallas_call | solution.py:120
  9.2 3.0 %collective-permute-start.2 = (bf16[128,2048]{1,0:T(8,128)(2,1)}, bf16[128,2048]{1,0:T(8,128)(2,1)S(1)}, u32[]{:S(2)}, u32[]{:S(2)}) collective-permute-start(bf16[128,2048]{1,0:T(8,128)(2,1)} %get-tuple-element.38), channel_id=1, source_target_pairs={{0,1},{1,0},{2,3},{3,2},{4,5},{5,4},{6,7},{7,6},{8,9},{9,8},{10,11... | collective-permute-start | bytes 1572872 | tf_op jit(solution)/shard_map/ppermute | solution.py:169
  12.5 0.9 fusion.9.pick_ref
  13.4 9.1 %shard_map.86 = (f32[256,2048]{1,0:T(8,128)}, bf16[256,2048]{1,0:T(8,128)(2,1)}, f32[128,2048]{1,0:T(8,128)}, bf16[128,2048]{1,0:T(8,128)(2,1)}) custom-call(bf16[384,512]{1,0:T(8,128)(2,1)} %fusion.9.pick_ref, bf16[2048,512]{1,0:T(8,128)(2,1)} %projector_ref.3, bf16[2048,2048]{1,0:T(8,128)(2,1)} %acts_ref.3), custom_call_target="tpu_custom_call" | custom-call | tf_op jit(solution)/shard_map/pallas_call | solution.py:120
  22.5 2.0 %collective-permute-start.1 = (bf16[128,2048]{1,0:T(8,128)(2,1)}, bf16[128,2048]{1,0:T(8,128)(2,1)}, u32[]{:S(2)}, u32[]{:S(2)}) collective-permute-start(bf16[128,2048]{1,0:T(8,128)(2,1)} %get-tuple-element.41), channel_id=1, source_target_pairs={{0,1},{1,0},{2,3},{3,2},{4,5},{5,4},{6,7},{7,6},{8,9},{9,8},{10,11... | collective-permute-start | bytes 1572872 | tf_op jit(solution)/shard_map/ppermute | solution.py:169
  24.6 1.0 constant_dynamic-slice_fusion
  25.7 11.5 %fusion.10 = f32[128,7168]{1,0:T(8,128)S(1)} fusion(bf16[2048,7168]{1,0:T(8,128)(2,1)} %param.7, f32[128,2048]{1,0:T(8,128)S(1)} %copy-done.2, bf16[128,2048]{1,0:T(8,128)(2,1)S(1)} %collective-permute-done.2), kind=kOutput, calls=%fused_computation.37 | convolution fusion | flops 3758882816 | bytes 34603008 | tf_op jit(solution)/shard_map/dot_general | solution.py:143
  37.2 1.8 copy-done
  39.0 1.0 slice.295
  40.8 2.0 %collective-permute-done.3 = bf16[64,7168]{1,0:T(8,128)(2,1)} collective-permute-done((bf16[64,7168]{1,0:T(8,128)(2,1)}, bf16[64,7168]{1,0:T(8,128)(2,1)}, u32[]{:S(2)}, u32[]{:S(2)}) %collective-permute-start.3) | collective-permute-done | bytes 917536 | tf_op jit(solution)/shard_map/ppermute | solution.py:165
  42.9 1.9 slice_add_fusion.2
  44.8 1.9 collective-permute-start.4
  46.7 2.0 %collective-permute-done.5 = bf16[256,2048]{1,0:T(8,128)(2,1)S(1)} collective-permute-done((bf16[256,2048]{1,0:T(8,128)(2,1)}, bf16[256,2048]{1,0:T(8,128)(2,1)S(1)}, u32[]{:S(2)}, u32[]{:S(2)}) %collective-permute-start.5) | collective-permute-done | bytes 1048608 | tf_op jit(solution)/shard_map/ppermute | solution.py:169
  49.1 7.3 %fusion.6 = f32[256,3584]{1,0:T(8,128)S(1)} fusion(bf16[256,2048]{1,0:T(8,128)(2,1)S(1)} %add_convert_fusion, bf16[2048,7168]{1,0:T(8,128)(2,1)} %param.7), kind=kOutput, calls=%fused_computation.6 | convolution fusion | flops 3758096384 | bytes 19398656 | tf_op jit(solution)/shard_map/dot_general | solution.py:143
  56.6 1.0 collective-permute-done.4
  57.7 1.9 collective-permute-start.6
  59.8 1.6 collective-permute-start.11
  61.4 7.3 %fusion.2 = f32[256,3584]{1,0:T(8,128)S(1)} fusion(bf16[256,2048]{1,0:T(8,128)(2,1)S(1)} %add_convert_fusion, bf16[2048,7168]{1,0:T(8,128)(2,1)} %param.7), kind=kOutput, calls=%fused_computation.2 | convolution fusion | flops 3758096384 | bytes 19398656 | tf_op jit(solution)/shard_map/dot_general | solution.py:143
  69.0 2.7 %collective-permute-start.9 = (bf16[8,7168]{1,0:T(8,128)(2,1)S(1)}, bf16[8,7168]{1,0:T(8,128)(2,1)S(1)}, u32[]{:S(2)}, u32[]{:S(2)}) collective-permute-start(bf16[8,7168]{1,0:T(8,128)(2,1)S(1)} %slice.310), channel_id=1, source_target_pairs={{0,16},{2,18},{4,20},{6,22},{8,24},{10,26},{12,28},{14,30},{16,0},... | collective-permute-start | bytes 344072 | tf_op jit(solution)/shard_map/ppermute | solution.py:165
  71.6 1.2 add_convert_fusion.1
  72.8 6.5 %fusion.4 = f32[128,3584]{1,0:T(8,128)S(1)} fusion(bf16[128,2048]{1,0:T(8,128)(2,1)S(1)} %add_convert_fusion.1, bf16[2048,7168]{1,0:T(8,128)(2,1)} %param.7), kind=kOutput, calls=%fused_computation.4 | convolution fusion | flops 1879048192 | bytes 17039360 | tf_op jit(solution)/shard_map/dot_general | solution.py:143
  80.5 6.4 %fusion = f32[128,3584]{1,0:T(8,128)S(1)} fusion(bf16[128,2048]{1,0:T(8,128)(2,1)S(1)} %add_convert_fusion.1, bf16[2048,7168]{1,0:T(8,128)(2,1)} %param.7), kind=kOutput, calls=%fused_computation | convolution fusion | flops 1879048192 | bytes 17039360 | tf_op jit(solution)/shard_map/dot_general | solution.py:143
  87.2 1.6 collective-permute-start.18
  88.9 1.1 collective-permute-start.13
  90.0 1.1 convolution_convert_fusion.basis_ref
  91.8 1.6 collective-permute-done.14
  93.5 1.1 collective-permute-start.16
  94.6 2.8 %collective-permute-done.13 = bf16[32,3584]{1,0:T(8,128)(2,1)S(1)} collective-permute-done((bf16[32,3584]{1,0:T(8,128)(2,1)S(1)}, bf16[32,3584]{1,0:T(8,128)(2,1)S(1)}, u32[]{:S(2)}, u32[]{:S(2)}) %collective-permute-start.13) | collective-permute-done | bytes 229408 | tf_op jit(solution)/shard_map/ppermute | solution.py:165
  97.5 0.9 collective-permute-start.15
  98.5 1.1 collective-permute-start.21
  99.6 2.9 %collective-permute-done.17 = bf16[32,3584]{1,0:T(8,128)(2,1)S(1)} collective-permute-done((bf16[32,3584]{1,0:T(8,128)(2,1)S(1)}, bf16[32,3584]{1,0:T(8,128)(2,1)S(1)}, u32[]{:S(2)}, u32[]{:S(2)}) %collective-permute-start.17) | collective-permute-done | bytes 229408 | tf_op jit(solution)/shard_map/ppermute | solution.py:165
  102.6 1.1 collective-permute-start.20
  103.7 0.8 collective-permute-done.16
  105.0 3.4 %collective-permute-done.21 = bf16[16,3584]{1,0:T(8,128)(2,1)S(1)} collective-permute-done((bf16[16,3584]{1,0:T(8,128)(2,1)S(1)}, bf16[16,3584]{1,0:T(8,128)(2,1)S(1)}, u32[]{:S(2)}, u32[]{:S(2)}) %collective-permute-start.21) | collective-permute-done | bytes 114720 | tf_op jit(solution)/shard_map/ppermute | solution.py:165
  108.6 2.1 %collective-permute-done.20 = bf16[16,3584]{1,0:T(8,128)(2,1)S(1)} collective-permute-done((bf16[16,3584]{1,0:T(8,128)(2,1)S(1)}, bf16[16,3584]{1,0:T(8,128)(2,1)S(1)}, u32[]{:S(2)}, u32[]{:S(2)}) %collective-permute-start.20) | collective-permute-done | bytes 114720 | tf_op jit(solution)/shard_map/ppermute | solution.py:165
  110.7 0.9 collective-permute-start.23
  111.6 4.2 %collective-permute-done.19 = bf16[16,3584]{1,0:T(8,128)(2,1)S(1)} collective-permute-done((bf16[16,3584]{1,0:T(8,128)(2,1)S(1)}, bf16[16,3584]{1,0:T(8,128)(2,1)S(1)}, u32[]{:S(2)}, u32[]{:S(2)}) %collective-permute-start.19) | collective-permute-done | bytes 114720 | tf_op jit(solution)/shard_map/ppermute | solution.py:165
  115.9 0.7 collective-permute-done.22
  117.5 10.9 %all_to_all.5 = f32[32,8,128]{2,1,0:T(8,128)S(1)} all-to-all(f32[32,8,128]{2,1,0:T(8,128)S(1)} %broadcast_in_dim.2), channel_id=1, replica_groups=mesh['dp'=16,'shard'=2] {'dp','shard'}, dimensions={0} | all-to-all | bytes 262144 | tf_op jit(solution)/shard_map/all_to_all | solution.py:273
  129.8 1.8 divide_convert_fusion
  131.7 0.7 collective-permute-start.47
  132.4 1.4 collective-permute-start.24
  133.8 0.7 collective-permute-start.33
  134.5 5.3 %collective-permute-done.24 = bf16[32,1024]{1,0:T(8,128)(2,1)S(1)} collective-permute-done((bf16[32,1024]{1,0:T(8,128)(2,1)S(1)}, bf16[32,1024]{1,0:T(8,128)(2,1)S(1)}, u32[]{:S(2)}, u32[]{:S(2)}) %collective-permute-start.24) | collective-permute-done | bytes 65568 | tf_op jit(solution)/shard_map/ppermute | solution.py:165
  139.8 0.7 collective-permute-start.32
  141.0 1.4 collective-permute-start.50
  142.5 6.6 %collective-permute-done.25.refs_1_ = bf16[64,1024]{1,0:T(8,128)(2,1)} collective-permute-done((bf16[64,1024]{1,0:T(8,128)(2,1)S(1)}, bf16[64,1024]{1,0:T(8,128)(2,1)}, u32[]{:S(2)}, u32[]{:S(2)}) %collective-permute-start.25) | collective-permute-done | bytes 131104 | tf_op jit(solution)/shard_map/ppermute | solution.py:298
  149.1 0.9 collective-permute-start.49
  150.5 5.6 %collective-permute-done.26.refs_2_ = bf16[64,1024]{1,0:T(8,128)(2,1)} collective-permute-done((bf16[64,1024]{1,0:T(8,128)(2,1)}, bf16[64,1024]{1,0:T(8,128)(2,1)}, u32[]{:S(2)}, u32[]{:S(2)}) %collective-permute-start.26) | collective-permute-done | bytes 131104 | tf_op jit(solution)/shard_map/ppermute | solution.py:298
  156.2 0.9 collective-permute-start.34
  157.6 7.1 %collective-permute-done.35.refs_4_ = bf16[32,3072]{1,0:T(8,128)(2,1)S(1)} collective-permute-done((bf16[32,3072]{1,0:T(8,128)(2,1)S(1)}, bf16[32,3072]{1,0:T(8,128)(2,1)S(1)}, u32[]{:S(2)}, u32[]{:S(2)}) %collective-permute-start.35) | collective-permute-done | bytes 196640 | tf_op jit(solution)/shard_map/ppermute | solution.py:302
  164.7 0.7 collective-permute-start.51
  165.9 1.7 collective-permute-done.27.refs_3_
  167.6 6.1 %collective-permute-done.52.refs_6_ = bf16[32,3072]{1,0:T(8,128)(2,1)S(1)} collective-permute-done((bf16[32,3072]{1,0:T(8,128)(2,1)S(1)}, bf16[32,3072]{1,0:T(8,128)(2,1)S(1)}, u32[]{:S(2)}, u32[]{:S(2)}) %collective-permute-start.52) | collective-permute-done | bytes 196640 | tf_op jit(solution)/shard_map/ppermute | solution.py:302
  174.3 1.9 collective-permute-start.53
  176.4 5.1 %collective-permute-done.36.refs_5_ = bf16[32,3072]{1,0:T(8,128)(2,1)S(1)} collective-permute-done((bf16[32,3072]{1,0:T(8,128)(2,1)S(1)}, bf16[32,3072]{1,0:T(8,128)(2,1)S(1)}, u32[]{:S(2)}, u32[]{:S(2)}) %collective-permute-start.36) | collective-permute-done | bytes 196640 | tf_op jit(solution)/shard_map/ppermute | solution.py:165
  182.1 3.5 %collective-permute-done.53.refs_7_ = bf16[32,3072]{1,0:T(8,128)(2,1)S(1)} collective-permute-done((bf16[32,3072]{1,0:T(8,128)(2,1)S(1)}, bf16[32,3072]{1,0:T(8,128)(2,1)S(1)}, u32[]{:S(2)}, u32[]{:S(2)}) %collective-permute-start.53) | collective-permute-done | bytes 196640 | tf_op jit(solution)/shard_map/ppermute | solution.py:165
  186.2 1.6 collective-permute-done.38.refs_7_
  189.0 0.7 copy-done.38
  189.8 4.0 %shard_map.87.refs_17_ = bf16[256,7168]{1,0:T(8,128)(2,1)} custom-call(bf16[256,512]{1,0:T(8,128)(2,1)} %convolution_convert_fusion.basis_ref, bf16[32,3072]{1,0:T(8,128)(2,1)} %copy-done.7, bf16[32,3072]{1,0:T(8,128)(2,1)} %copy-done.25, bf16[32,3072]{1,0:T(8,128)(2,1)} %copy-done.24, bf16[32,3072]{1,0:T(8,128)(2,1)} %copy-done.28, ...), custom_call_target="tpu_custom_call" | custom-call | tf_op jit(solution)/shard_map/pallas_call | solution.py:65
  194.0 0.7 copy-done.23
  194.6 4.0 %shard_map.88.refs_9_ = bf16[256,7168]{1,0:T(8,128)(2,1)} custom-call(bf16[256,512]{1,0:T(8,128)(2,1)} %convolution_convert_fusion.basis_ref, bf16[32,3072]{1,0:T(8,128)(2,1)} %copy-done.6, bf16[32,3072]{1,0:T(8,128)(2,1)} %copy-done.10, bf16[32,3072]{1,0:T(8,128)(2,1)} %copy-done.9, bf16[32,3072]{1,0:T(8,128)(2,1)} %copy-done.13, ...), custom_call_target="tpu_custom_call", output_to_operand_aliasing={{}: (18, {})} | custom-call | tf_op jit(solution)/shard_map/pallas_call | solution.py:65
  198.7 2.8 %shard_map.89 = bf16[256,7168]{1,0:T(8,128)(2,1)} custom-call(bf16[256,512]{1,0:T(8,128)(2,1)} %convolution_convert_fusion.basis_ref, bf16[64,1024]{1,0:T(8,128)(2,1)} %copy-done.8, bf16[64,1024]{1,0:T(8,128)(2,1)} %collective-permute-done.25.refs_1_, bf16[64,1024]{1,0:T(8,128)(2,1)} %collective-permute-done.26.refs_2_, ...), custom_call_target="tpu_custom_call", output_to_operand_aliasing={{}: (10, {})} | custom-call | tf_op jit(solution)/shard_map/pallas_call | solution.py:65
  (223 shorter events, 12.2 us)
Async XLA Ops:
  9.2 16.5 %collective-permute-start.2 = (bf16[128,2048]{1,0:T(8,128)(2,1)}, bf16[128,2048]{1,0:T(8,128)(2,1)S(1)}, u32[]{:S(2)}, u32[]{:S(2)}) collective-permute-start(bf16[128,2048]{1,0:T(8,128)(2,1)} %get-tuple-element.38), channel_id=1, source_target_pairs={{0,1},{1,0},{2,3},{3,2},{4,5},{5,4},{6,7},{7,6},{8,9},{9,8},{10,11... | collective-permute-start | bytes 1572872 | tf_op jit(solution)/shard_map/ppermute | solution.py:169
  22.5 26.2 %collective-permute-start.5 = (bf16[256,2048]{1,0:T(8,128)(2,1)}, bf16[256,2048]{1,0:T(8,128)(2,1)S(1)}, u32[]{:S(2)}, u32[]{:S(2)}) collective-permute-start(bf16[256,2048]{1,0:T(8,128)(2,1)} %get-tuple-element.43), channel_id=1, source_target_pairs={{0,1},{1,0},{2,3},{3,2},{4,5},{5,4},{6,7},{7,6},{8,9},{9,8},{10,11... | collective-permute-start | bytes 3145736 | tf_op jit(solution)/shard_map/ppermute | solution.py:169
  22.5 49.1 %collective-permute-start.1 = (bf16[128,2048]{1,0:T(8,128)(2,1)}, bf16[128,2048]{1,0:T(8,128)(2,1)}, u32[]{:S(2)}, u32[]{:S(2)}) collective-permute-start(bf16[128,2048]{1,0:T(8,128)(2,1)} %get-tuple-element.41), channel_id=1, source_target_pairs={{0,1},{1,0},{2,3},{3,2},{4,5},{5,4},{6,7},{7,6},{8,9},{9,8},{10,11... | collective-permute-start | bytes 1572872 | tf_op jit(solution)/shard_map/ppermute | solution.py:169
  25.5 63.3 %collective-permute-start = (bf16[256,512]{1,0:T(8,128)(2,1)S(1)}, bf16[256,512]{1,0:T(8,128)(2,1)}, u32[]{:S(2)}, u32[]{:S(2)}) collective-permute-start(bf16[256,512]{1,0:T(8,128)(2,1)S(1)} %constant_dynamic-slice_fusion), channel_id=1, source_target_pairs={{0,1},{1,0},{2,3},{3,2},{4,5},{5,4},{6,7},{7,6},{8,9},{9,8},{10,11... | collective-permute-start | bytes 786440 | tf_op jit(solution)/shard_map/ppermute | solution.py:210
  40.0 2.8 %collective-permute-start.3 = (bf16[64,7168]{1,0:T(8,128)(2,1)}, bf16[64,7168]{1,0:T(8,128)(2,1)}, u32[]{:S(2)}, u32[]{:S(2)}) collective-permute-start(bf16[64,7168]{1,0:T(8,128)(2,1)} %slice.295), channel_id=1, source_target_pairs={{0,2},{2,0},{4,6},{6,4},{8,10},{10,8},{12,14},{14,12},{16,18},{18,... | collective-permute-start | bytes 2752520 | tf_op jit(solution)/shard_map/ppermute | solution.py:165
  44.8 12.8 %collective-permute-start.4 = (bf16[32,7168]{1,0:T(8,128)(2,1)S(1)}, bf16[32,7168]{1,0:T(8,128)(2,1)S(1)}, u32[]{:S(2)}, u32[]{:S(2)}) collective-permute-start(bf16[32,7168]{1,0:T(8,128)(2,1)S(1)} %slice.300), channel_id=1, source_target_pairs={{0,4},{2,6},{4,0},{6,2},{8,12},{10,14},{12,8},{14,10},{16,20},{18,... | collective-permute-start | bytes 1376264 | tf_op jit(solution)/shard_map/ppermute | solution.py:165
  56.5 3.1 %collective-permute-start.7 = (bf16[128,3584]{1,0:T(8,128)(2,1)S(1)}, bf16[128,3584]{1,0:T(8,128)(2,1)S(1)}, u32[]{:S(2)}, u32[]{:S(2)}) collective-permute-start(bf16[128,3584]{1,0:T(8,128)(2,1)S(1)} %slice.294), channel_id=1, source_target_pairs={{0,2},{2,0},{4,6},{6,4},{8,10},{10,8},{12,14},{14,12},{16,18},{18,... | collective-permute-start | bytes 2752520 | tf_op jit(solution)/shard_map/ppermute | solution.py:165
  57.7 11.2 %collective-permute-start.6 = (bf16[16,7168]{1,0:T(8,128)(2,1)S(1)}, bf16[16,7168]{1,0:T(8,128)(2,1)S(1)}, u32[]{:S(2)}, u32[]{:S(2)}) collective-permute-start(bf16[16,7168]{1,0:T(8,128)(2,1)S(1)} %slice.305), channel_id=1, source_target_pairs={{0,8},{2,10},{4,12},{6,14},{8,0},{10,2},{12,4},{14,6},{16,24},{18,... | collective-permute-start | bytes 688136 | tf_op jit(solution)/shard_map/ppermute | solution.py:165
  59.8 27.4 %collective-permute-start.11 = (bf16[64,3584]{1,0:T(8,128)(2,1)S(1)}, bf16[64,3584]{1,0:T(8,128)(2,1)S(1)}, u32[]{:S(2)}, u32[]{:S(2)}) collective-permute-start(bf16[64,3584]{1,0:T(8,128)(2,1)S(1)} %slice.299), channel_id=1, source_target_pairs={{0,4},{2,6},{4,0},{6,2},{8,12},{10,14},{12,8},{14,10},{16,20},{18,... | collective-permute-start | bytes 1376264 | tf_op jit(solution)/shard_map/ppermute | solution.py:165
  68.8 10.9 %collective-permute-start.8 = (bf16[128,3584]{1,0:T(8,128)(2,1)S(1)}, bf16[128,3584]{1,0:T(8,128)(2,1)S(1)}, u32[]{:S(2)}, u32[]{:S(2)}) collective-permute-start(bf16[128,3584]{1,0:T(8,128)(2,1)S(1)} %slice.293), channel_id=1, source_target_pairs={{0,2},{2,0},{4,6},{6,4},{8,10},{10,8},{12,14},{14,12},{16,18},{18,... | collective-permute-start | bytes 2752520 | tf_op jit(solution)/shard_map/ppermute | solution.py:165
  69.0 22.8 %collective-permute-start.9 = (bf16[8,7168]{1,0:T(8,128)(2,1)S(1)}, bf16[8,7168]{1,0:T(8,128)(2,1)S(1)}, u32[]{:S(2)}, u32[]{:S(2)}) collective-permute-start(bf16[8,7168]{1,0:T(8,128)(2,1)S(1)} %slice.310), channel_id=1, source_target_pairs={{0,16},{2,18},{4,20},{6,22},{8,24},{10,26},{12,28},{14,30},{16,0},... | collective-permute-start | bytes 344072 | tf_op jit(solution)/shard_map/ppermute | solution.py:165
  79.4 7.5 %collective-permute-start.12 = (bf16[64,3584]{1,0:T(8,128)(2,1)S(1)}, bf16[64,3584]{1,0:T(8,128)(2,1)S(1)}, u32[]{:S(2)}, u32[]{:S(2)}) collective-permute-start(bf16[64,3584]{1,0:T(8,128)(2,1)S(1)} %slice.298), channel_id=1, source_target_pairs={{0,2},{2,0},{4,6},{6,4},{8,10},{10,8},{12,14},{14,12},{16,18},{18,... | collective-permute-start | bytes 1376264 | tf_op jit(solution)/shard_map/ppermute | solution.py:165
  79.9 13.5 %collective-permute-start.14 = (bf16[64,3584]{1,0:T(8,128)(2,1)S(1)}, bf16[64,3584]{1,0:T(8,128)(2,1)S(1)}, u32[]{:S(2)}, u32[]{:S(2)}) collective-permute-start(bf16[64,3584]{1,0:T(8,128)(2,1)S(1)} %slice.297), channel_id=1, source_target_pairs={{0,4},{2,6},{4,0},{6,2},{8,12},{10,14},{12,8},{14,10},{16,20},{18,... | collective-permute-start | bytes 1376264 | tf_op jit(solution)/shard_map/ppermute | solution.py:165
  87.0 4.1 %collective-permute-start.10 = (bf16[64,3584]{1,0:T(8,128)(2,1)S(1)}, bf16[64,3584]{1,0:T(8,128)(2,1)S(1)}, u32[]{:S(2)}, u32[]{:S(2)}) collective-permute-start(bf16[64,3584]{1,0:T(8,128)(2,1)S(1)} %slice.296), channel_id=1, source_target_pairs={{0,2},{2,0},{4,6},{6,4},{8,10},{10,8},{12,14},{14,12},{16,18},{18,... | collective-permute-start | bytes 1376264 | tf_op jit(solution)/shard_map/ppermute | solution.py:165
  87.2 11.2 %collective-permute-start.18 = (bf16[32,3584]{1,0:T(8,128)(2,1)S(1)}, bf16[32,3584]{1,0:T(8,128)(2,1)S(1)}, u32[]{:S(2)}, u32[]{:S(2)}) collective-permute-start(bf16[32,3584]{1,0:T(8,128)(2,1)S(1)} %slice.304), channel_id=1, source_target_pairs={{0,4},{2,6},{4,0},{6,2},{8,12},{10,14},{12,8},{14,10},{16,20},{18,... | collective-permute-start | bytes 688136 | tf_op jit(solution)/shard_map/ppermute | solution.py:165
  88.9 8.5 %collective-permute-start.13 = (bf16[32,3584]{1,0:T(8,128)(2,1)S(1)}, bf16[32,3584]{1,0:T(8,128)(2,1)S(1)}, u32[]{:S(2)}, u32[]{:S(2)}) collective-permute-start(bf16[32,3584]{1,0:T(8,128)(2,1)S(1)} %slice.303), channel_id=1, source_target_pairs={{0,8},{2,10},{4,12},{6,14},{8,0},{10,2},{12,4},{14,6},{16,24},{18,... | collective-permute-start | bytes 688136 | tf_op jit(solution)/shard_map/ppermute | solution.py:165
  91.2 11.4 %collective-permute-start.17 = (bf16[32,3584]{1,0:T(8,128)(2,1)S(1)}, bf16[32,3584]{1,0:T(8,128)(2,1)S(1)}, u32[]{:S(2)}, u32[]{:S(2)}) collective-permute-start(bf16[32,3584]{1,0:T(8,128)(2,1)S(1)} %slice.302), channel_id=1, source_target_pairs={{0,4},{2,6},{4,0},{6,2},{8,12},{10,14},{12,8},{14,10},{16,20},{18,... | collective-permute-start | bytes 688136 | tf_op jit(solution)/shard_map/ppermute | solution.py:165
  93.5 11.0 %collective-permute-start.16 = (bf16[32,3584]{1,0:T(8,128)(2,1)S(1)}, bf16[32,3584]{1,0:T(8,128)(2,1)S(1)}, u32[]{:S(2)}, u32[]{:S(2)}) collective-permute-start(bf16[32,3584]{1,0:T(8,128)(2,1)S(1)} %slice.301), channel_id=1, source_target_pairs={{0,8},{2,10},{4,12},{6,14},{8,0},{10,2},{12,4},{14,6},{16,24},{18,... | collective-permute-start | bytes 688136 | tf_op jit(solution)/shard_map/ppermute | solution.py:165
  97.5 7.5 %collective-permute-start.15 = (bf16[16,3584]{1,0:T(8,128)(2,1)S(1)}, bf16[16,3584]{1,0:T(8,128)(2,1)S(1)}, u32[]{:S(2)}, u32[]{:S(2)}) collective-permute-start(bf16[16,3584]{1,0:T(8,128)(2,1)S(1)} %slice.309), channel_id=1, source_target_pairs={{0,16},{2,18},{4,20},{6,22},{8,24},{10,26},{12,28},{14,30},{16,0},... | collective-permute-start | bytes 344072 | tf_op jit(solution)/shard_map/ppermute | solution.py:165
  98.5 10.0 %collective-permute-start.21 = (bf16[16,3584]{1,0:T(8,128)(2,1)S(1)}, bf16[16,3584]{1,0:T(8,128)(2,1)S(1)}, u32[]{:S(2)}, u32[]{:S(2)}) collective-permute-start(bf16[16,3584]{1,0:T(8,128)(2,1)S(1)} %slice.308), channel_id=1, source_target_pairs={{0,8},{2,10},{4,12},{6,14},{8,0},{10,2},{12,4},{14,6},{16,24},{18,... | collective-permute-start | bytes 344072 | tf_op jit(solution)/shard_map/ppermute | solution.py:165
  102.6 8.1 %collective-permute-start.20 = (bf16[16,3584]{1,0:T(8,128)(2,1)S(1)}, bf16[16,3584]{1,0:T(8,128)(2,1)S(1)}, u32[]{:S(2)}, u32[]{:S(2)}) collective-permute-start(bf16[16,3584]{1,0:T(8,128)(2,1)S(1)} %slice.307), channel_id=1, source_target_pairs={{0,8},{2,10},{4,12},{6,14},{8,0},{10,2},{12,4},{14,6},{16,24},{18,... | collective-permute-start | bytes 344072 | tf_op jit(solution)/shard_map/ppermute | solution.py:165
  104.6 11.2 %collective-permute-start.19 = (bf16[16,3584]{1,0:T(8,128)(2,1)S(1)}, bf16[16,3584]{1,0:T(8,128)(2,1)S(1)}, u32[]{:S(2)}, u32[]{:S(2)}) collective-permute-start(bf16[16,3584]{1,0:T(8,128)(2,1)S(1)} %slice.306), channel_id=1, source_target_pairs={{0,16},{2,18},{4,20},{6,22},{8,24},{10,26},{12,28},{14,30},{16,0},... | collective-permute-start | bytes 344072 | tf_op jit(solution)/shard_map/ppermute | solution.py:165
  108.5 8.1 %collective-permute-start.22 = (bf16[8,3584]{1,0:T(8,128)(2,1)S(1)}, bf16[8,3584]{1,0:T(8,128)(2,1)S(1)}, u32[]{:S(2)}, u32[]{:S(2)}) collective-permute-start(bf16[8,3584]{1,0:T(8,128)(2,1)S(1)} %slice.312), channel_id=1, source_target_pairs={{0,16},{2,18},{4,20},{6,22},{8,24},{10,26},{12,28},{14,30},{16,0},... | collective-permute-start | bytes 172040 | tf_op jit(solution)/shard_map/ppermute | solution.py:165
  110.7 6.5 %collective-permute-start.23 = (bf16[8,3584]{1,0:T(8,128)(2,1)S(1)}, bf16[8,3584]{1,0:T(8,128)(2,1)S(1)}, u32[]{:S(2)}, u32[]{:S(2)}) collective-permute-start(bf16[8,3584]{1,0:T(8,128)(2,1)S(1)} %slice.311), channel_id=1, source_target_pairs={{0,16},{2,18},{4,20},{6,22},{8,24},{10,26},{12,28},{14,30},{16,0},... | collective-permute-start | bytes 172040 | tf_op jit(solution)/shard_map/ppermute | solution.py:165
  131.6 58.1 %copy-start.7 = (bf16[32,3072]{1,0:T(8,128)(2,1)}, bf16[32,3072]{1,0:T(8,128)(2,1)S(1)}, u32[]{:S(2)}) copy-start(bf16[32,3072]{1,0:T(8,128)(2,1)S(1)} %get-tuple-element.76.refs_0_) | copy-start | bytes 589828
  131.6 62.2 %copy-start.6 = (bf16[32,3072]{1,0:T(8,128)(2,1)}, bf16[32,3072]{1,0:T(8,128)(2,1)S(1)}, u32[]{:S(2)}) copy-start(bf16[32,3072]{1,0:T(8,128)(2,1)S(1)} %get-tuple-element.77.refs_0_) | copy-start | bytes 589828
  131.6 9.2 %collective-permute-start.48 = (bf16[32,3072]{1,0:T(8,128)(2,1)S(1)}, bf16[32,3072]{1,0:T(8,128)(2,1)S(1)}, u32[]{:S(2)}, u32[]{:S(2)}) collective-permute-start(bf16[32,3072]{1,0:T(8,128)(2,1)S(1)} %get-tuple-element.76.refs_0_), channel_id=1, source_target_pairs={{0,8},{2,10},{4,12},{6,14},{8,16},{10,18},{12,20},{14,22},{16,24},... | collective-permute-start | bytes 589832 | tf_op jit(solution)/shard_map/ppermute | solution.py:302
  131.7 9.3 %collective-permute-start.47 = (bf16[32,3072]{1,0:T(8,128)(2,1)S(1)}, bf16[32,3072]{1,0:T(8,128)(2,1)S(1)}, u32[]{:S(2)}, u32[]{:S(2)}) collective-permute-start(bf16[32,3072]{1,0:T(8,128)(2,1)S(1)} %get-tuple-element.76.refs_0_), channel_id=1, source_target_pairs={{0,4},{2,6},{4,0},{6,2},{8,12},{10,14},{12,8},{14,10},{16,20},{18,... | collective-permute-start | bytes 589832 | tf_op jit(solution)/shard_map/ppermute | solution.py:165
  132.4 7.4 %collective-permute-start.24 = (bf16[32,1024]{1,0:T(8,128)(2,1)S(1)}, bf16[32,1024]{1,0:T(8,128)(2,1)S(1)}, u32[]{:S(2)}, u32[]{:S(2)}) collective-permute-start(bf16[32,1024]{1,0:T(8,128)(2,1)S(1)} %slice.242), channel_id=1, source_target_pairs={{0,4},{2,6},{4,0},{6,2},{8,12},{10,14},{12,8},{14,10},{16,20},{18,... | collective-permute-start | bytes 196616 | tf_op jit(solution)/shard_map/ppermute | solution.py:165
  133.8 7.2 %collective-permute-start.54 = (bf16[32,3072]{1,0:T(8,128)(2,1)S(1)}, bf16[32,3072]{1,0:T(8,128)(2,1)S(1)}, u32[]{:S(2)}, u32[]{:S(2)}) collective-permute-start(bf16[32,3072]{1,0:T(8,128)(2,1)S(1)} %get-tuple-element.76.refs_0_), channel_id=1, source_target_pairs={{0,2},{2,0},{4,6},{6,4},{8,10},{10,8},{12,14},{14,12},{16,18},{18,... | collective-permute-start | bytes 589832 | tf_op jit(solution)/shard_map/ppermute | solution.py:165
  133.8 15.3 %collective-permute-start.33 = (bf16[32,3072]{1,0:T(8,128)(2,1)S(1)}, bf16[32,3072]{1,0:T(8,128)(2,1)S(1)}, u32[]{:S(2)}, u32[]{:S(2)}) collective-permute-start(bf16[32,3072]{1,0:T(8,128)(2,1)S(1)} %get-tuple-element.77.refs_0_), channel_id=1, source_target_pairs={{0,8},{2,10},{4,12},{6,14},{8,16},{10,18},{12,20},{14,22},{16,24},... | collective-permute-start | bytes 589832 | tf_op jit(solution)/shard_map/ppermute | solution.py:302
  139.8 10.2 %collective-permute-start.32 = (bf16[32,3072]{1,0:T(8,128)(2,1)S(1)}, bf16[32,3072]{1,0:T(8,128)(2,1)S(1)}, u32[]{:S(2)}, u32[]{:S(2)}) collective-permute-start(bf16[32,3072]{1,0:T(8,128)(2,1)S(1)} %get-tuple-element.77.refs_0_), channel_id=1, source_target_pairs={{0,4},{2,6},{4,0},{6,2},{8,12},{10,14},{12,8},{14,10},{16,20},{18,... | collective-permute-start | bytes 589832 | tf_op jit(solution)/shard_map/ppermute | solution.py:165
  140.8 8.3 %collective-permute-start.25 = (bf16[64,1024]{1,0:T(8,128)(2,1)S(1)}, bf16[64,1024]{1,0:T(8,128)(2,1)}, u32[]{:S(2)}, u32[]{:S(2)}) collective-permute-start(bf16[64,1024]{1,0:T(8,128)(2,1)S(1)} %pad_maximum_fusion.refs_0_), channel_id=1, source_target_pairs={{0,8},{2,10},{4,12},{6,14},{8,16},{10,18},{12,20},{14,22},{16,24},... | collective-permute-start | bytes 393224 | tf_op jit(solution)/shard_map/ppermute | solution.py:298
  141.0 9.0 %collective-permute-start.39 = (bf16[32,3072]{1,0:T(8,128)(2,1)S(1)}, bf16[32,3072]{1,0:T(8,128)(2,1)S(1)}, u32[]{:S(2)}, u32[]{:S(2)}) collective-permute-start(bf16[32,3072]{1,0:T(8,128)(2,1)S(1)} %get-tuple-element.77.refs_0_), channel_id=1, source_target_pairs={{0,2},{2,0},{4,6},{6,4},{8,10},{10,8},{12,14},{14,12},{16,18},{18,... | collective-permute-start | bytes 589832 | tf_op jit(solution)/shard_map/ppermute | solution.py:165
  141.0 15.1 %collective-permute-start.50 = (bf16[32,3072]{1,0:T(8,128)(2,1)S(1)}, bf16[32,3072]{1,0:T(8,128)(2,1)S(1)}, u32[]{:S(2)}, u32[]{:S(2)}) collective-permute-start(bf16[32,3072]{1,0:T(8,128)(2,1)S(1)} %collective-permute-done.48.refs_2_), channel_id=1, source_target_pairs={{0,8},{2,10},{4,12},{6,14},{8,16},{10,18},{12,20},{14,22},{16,24},... | collective-permute-start | bytes 589832 | tf_op jit(solution)/shard_map/ppermute | solution.py:302
  149.1 7.1 %collective-permute-start.26 = (bf16[64,1024]{1,0:T(8,128)(2,1)}, bf16[64,1024]{1,0:T(8,128)(2,1)}, u32[]{:S(2)}, u32[]{:S(2)}) collective-permute-start(bf16[64,1024]{1,0:T(8,128)(2,1)} %collective-permute-done.25.refs_1_), channel_id=1, source_target_pairs={{0,8},{2,10},{4,12},{6,14},{8,16},{10,18},{12,20},{14,22},{16,24},... | collective-permute-start | bytes 393224 | tf_op jit(solution)/shard_map/ppermute | solution.py:298
  149.1 8.0 %collective-permute-start.49 = (bf16[32,3072]{1,0:T(8,128)(2,1)S(1)}, bf16[32,3072]{1,0:T(8,128)(2,1)S(1)}, u32[]{:S(2)}, u32[]{:S(2)}) collective-permute-start(bf16[32,3072]{1,0:T(8,128)(2,1)S(1)} %collective-permute-done.48.refs_2_), channel_id=1, source_target_pairs={{0,4},{2,6},{4,0},{6,2},{8,12},{10,14},{12,8},{14,10},{16,20},{18,... | collective-permute-start | bytes 589832 | tf_op jit(solution)/shard_map/ppermute | solution.py:165
  150.0 7.1 %collective-permute-start.55 = (bf16[32,3072]{1,0:T(8,128)(2,1)S(1)}, bf16[32,3072]{1,0:T(8,128)(2,1)S(1)}, u32[]{:S(2)}, u32[]{:S(2)}) collective-permute-start(bf16[32,3072]{1,0:T(8,128)(2,1)S(1)} %collective-permute-done.47.refs_1_), channel_id=1, source_target_pairs={{0,2},{2,0},{4,6},{6,4},{8,10},{10,8},{12,14},{14,12},{16,18},{18,... | collective-permute-start | bytes 589832 | tf_op jit(solution)/shard_map/ppermute | solution.py:165
  150.1 7.6 %collective-permute-start.56 = (bf16[32,3072]{1,0:T(8,128)(2,1)S(1)}, bf16[32,3072]{1,0:T(8,128)(2,1)S(1)}, u32[]{:S(2)}, u32[]{:S(2)}) collective-permute-start(bf16[32,3072]{1,0:T(8,128)(2,1)S(1)} %collective-permute-done.48.refs_2_), channel_id=1, source_target_pairs={{0,2},{2,0},{4,6},{6,4},{8,10},{10,8},{12,14},{14,12},{16,18},{18,... | collective-permute-start | bytes 589832 | tf_op jit(solution)/shard_map/ppermute | solution.py:165
  156.1 8.5 %collective-permute-start.35 = (bf16[32,3072]{1,0:T(8,128)(2,1)S(1)}, bf16[32,3072]{1,0:T(8,128)(2,1)S(1)}, u32[]{:S(2)}, u32[]{:S(2)}) collective-permute-start(bf16[32,3072]{1,0:T(8,128)(2,1)S(1)} %collective-permute-done.33.refs_2_), channel_id=1, source_target_pairs={{0,8},{2,10},{4,12},{6,14},{8,16},{10,18},{12,20},{14,22},{16,24},... | collective-permute-start | bytes 589832 | tf_op jit(solution)/shard_map/ppermute | solution.py:302
  156.2 8.5 %collective-permute-start.34 = (bf16[32,3072]{1,0:T(8,128)(2,1)S(1)}, bf16[32,3072]{1,0:T(8,128)(2,1)S(1)}, u32[]{:S(2)}, u32[]{:S(2)}) collective-permute-start(bf16[32,3072]{1,0:T(8,128)(2,1)S(1)} %collective-permute-done.33.refs_2_), channel_id=1, source_target_pairs={{0,4},{2,6},{4,0},{6,2},{8,12},{10,14},{12,8},{14,10},{16,20},{18,... | collective-permute-start | bytes 589832 | tf_op jit(solution)/shard_map/ppermute | solution.py:165
  157.1 8.3 %collective-permute-start.40 = (bf16[32,3072]{1,0:T(8,128)(2,1)S(1)}, bf16[32,3072]{1,0:T(8,128)(2,1)S(1)}, u32[]{:S(2)}, u32[]{:S(2)}) collective-permute-start(bf16[32,3072]{1,0:T(8,128)(2,1)S(1)} %collective-permute-done.32.refs_1_), channel_id=1, source_target_pairs={{0,2},{2,0},{4,6},{6,4},{8,10},{10,8},{12,14},{14,12},{16,18},{18,... | collective-permute-start | bytes 589832 | tf_op jit(solution)/shard_map/ppermute | solution.py:165
  157.1 8.3 %collective-permute-start.41 = (bf16[32,3072]{1,0:T(8,128)(2,1)S(1)}, bf16[32,3072]{1,0:T(8,128)(2,1)S(1)}, u32[]{:S(2)}, u32[]{:S(2)}) collective-permute-start(bf16[32,3072]{1,0:T(8,128)(2,1)S(1)} %collective-permute-done.33.refs_2_), channel_id=1, source_target_pairs={{0,2},{2,0},{4,6},{6,4},{8,10},{10,8},{12,14},{14,12},{16,18},{18,... | collective-permute-start | bytes 589832 | tf_op jit(solution)/shard_map/ppermute | solution.py:165
  157.6 10.0 %collective-permute-start.27 = (bf16[64,1024]{1,0:T(8,128)(2,1)}, bf16[64,1024]{1,0:T(8,128)(2,1)}, u32[]{:S(2)}, u32[]{:S(2)}) collective-permute-start(bf16[64,1024]{1,0:T(8,128)(2,1)} %collective-permute-done.26.refs_2_), channel_id=1, source_target_pairs={{0,8},{2,10},{4,12},{6,14},{8,16},{10,18},{12,20},{14,22},{16,24},... | collective-permute-start | bytes 393224 | tf_op jit(solution)/shard_map/ppermute | solution.py:298
  164.7 9.0 %collective-permute-start.52 = (bf16[32,3072]{1,0:T(8,128)(2,1)S(1)}, bf16[32,3072]{1,0:T(8,128)(2,1)S(1)}, u32[]{:S(2)}, u32[]{:S(2)}) collective-permute-start(bf16[32,3072]{1,0:T(8,128)(2,1)S(1)} %collective-permute-done.50.refs_4_), channel_id=1, source_target_pairs={{0,8},{2,10},{4,12},{6,14},{8,16},{10,18},{12,20},{14,22},{16,24},... | collective-permute-start | bytes 589832 | tf_op jit(solution)/shard_map/ppermute | solution.py:302
  164.7 9.0 %collective-permute-start.51 = (bf16[32,3072]{1,0:T(8,128)(2,1)S(1)}, bf16[32,3072]{1,0:T(8,128)(2,1)S(1)}, u32[]{:S(2)}, u32[]{:S(2)}) collective-permute-start(bf16[32,3072]{1,0:T(8,128)(2,1)S(1)} %collective-permute-done.50.refs_4_), channel_id=1, source_target_pairs={{0,4},{2,6},{4,0},{6,2},{8,12},{10,14},{12,8},{14,10},{16,20},{18,... | collective-permute-start | bytes 589832 | tf_op jit(solution)/shard_map/ppermute | solution.py:165
  165.4 8.4 %collective-permute-start.57 = (bf16[32,3072]{1,0:T(8,128)(2,1)S(1)}, bf16[32,3072]{1,0:T(8,128)(2,1)S(1)}, u32[]{:S(2)}, u32[]{:S(2)}) collective-permute-start(bf16[32,3072]{1,0:T(8,128)(2,1)S(1)} %collective-permute-done.49.refs_3_), channel_id=1, source_target_pairs={{0,2},{2,0},{4,6},{6,4},{8,10},{10,8},{12,14},{14,12},{16,18},{18,... | collective-permute-start | bytes 589832 | tf_op jit(solution)/shard_map/ppermute | solution.py:165
  165.4 8.9 %collective-permute-start.58 = (bf16[32,3072]{1,0:T(8,128)(2,1)S(1)}, bf16[32,3072]{1,0:T(8,128)(2,1)S(1)}, u32[]{:S(2)}, u32[]{:S(2)}) collective-permute-start(bf16[32,3072]{1,0:T(8,128)(2,1)S(1)} %collective-permute-done.50.refs_4_), channel_id=1, source_target_pairs={{0,2},{2,0},{4,6},{6,4},{8,10},{10,8},{12,14},{14,12},{16,18},{18,... | collective-permute-start | bytes 589832 | tf_op jit(solution)/shard_map/ppermute | solution.py:165
  167.6 8.8 %collective-permute-start.37 = (bf16[32,3072]{1,0:T(8,128)(2,1)S(1)}, bf16[32,3072]{1,0:T(8,128)(2,1)S(1)}, u32[]{:S(2)}, u32[]{:S(2)}) collective-permute-start(bf16[32,3072]{1,0:T(8,128)(2,1)S(1)} %collective-permute-done.35.refs_4_), channel_id=1, source_target_pairs={{0,8},{2,10},{4,12},{6,14},{8,16},{10,18},{12,20},{14,22},{16,24},... | collective-permute-start | bytes 589832 | tf_op jit(solution)/shard_map/ppermute | solution.py:302
  173.7 7.8 %collective-permute-start.36 = (bf16[32,3072]{1,0:T(8,128)(2,1)S(1)}, bf16[32,3072]{1,0:T(8,128)(2,1)S(1)}, u32[]{:S(2)}, u32[]{:S(2)}) collective-permute-start(bf16[32,3072]{1,0:T(8,128)(2,1)S(1)} %collective-permute-done.35.refs_4_), channel_id=1, source_target_pairs={{0,4},{2,6},{4,0},{6,2},{8,12},{10,14},{12,8},{14,10},{16,20},{18,... | collective-permute-start | bytes 589832 | tf_op jit(solution)/shard_map/ppermute | solution.py:165
  173.8 7.8 %collective-permute-start.42 = (bf16[32,3072]{1,0:T(8,128)(2,1)S(1)}, bf16[32,3072]{1,0:T(8,128)(2,1)S(1)}, u32[]{:S(2)}, u32[]{:S(2)}) collective-permute-start(bf16[32,3072]{1,0:T(8,128)(2,1)S(1)} %collective-permute-done.34.refs_3_), channel_id=1, source_target_pairs={{0,2},{2,0},{4,6},{6,4},{8,10},{10,8},{12,14},{14,12},{16,18},{18,... | collective-permute-start | bytes 589832 | tf_op jit(solution)/shard_map/ppermute | solution.py:165
  173.9 7.8 %collective-permute-start.43 = (bf16[32,3072]{1,0:T(8,128)(2,1)S(1)}, bf16[32,3072]{1,0:T(8,128)(2,1)S(1)}, u32[]{:S(2)}, u32[]{:S(2)}) collective-permute-start(bf16[32,3072]{1,0:T(8,128)(2,1)S(1)} %collective-permute-done.35.refs_4_), channel_id=1, source_target_pairs={{0,2},{2,0},{4,6},{6,4},{8,10},{10,8},{12,14},{14,12},{16,18},{18,... | collective-permute-start | bytes 589832 | tf_op jit(solution)/shard_map/ppermute | solution.py:165
  174.3 11.3 %collective-permute-start.53 = (bf16[32,3072]{1,0:T(8,128)(2,1)S(1)}, bf16[32,3072]{1,0:T(8,128)(2,1)S(1)}, u32[]{:S(2)}, u32[]{:S(2)}) collective-permute-start(bf16[32,3072]{1,0:T(8,128)(2,1)S(1)} %collective-permute-done.52.refs_6_), channel_id=1, source_target_pairs={{0,4},{2,6},{4,0},{6,2},{8,12},{10,14},{12,8},{14,10},{16,20},{18,... | collective-permute-start | bytes 589832 | tf_op jit(solution)/shard_map/ppermute | solution.py:165
  176.4 9.3 %collective-permute-start.59 = (bf16[32,3072]{1,0:T(8,128)(2,1)S(1)}, bf16[32,3072]{1,0:T(8,128)(2,1)S(1)}, u32[]{:S(2)}, u32[]{:S(2)}) collective-permute-start(bf16[32,3072]{1,0:T(8,128)(2,1)S(1)} %collective-permute-done.51.refs_5_), channel_id=1, source_target_pairs={{0,2},{2,0},{4,6},{6,4},{8,10},{10,8},{12,14},{14,12},{16,18},{18,... | collective-permute-start | bytes 589832 | tf_op jit(solution)/shard_map/ppermute | solution.py:165
  181.5 6.3 %collective-permute-start.38 = (bf16[32,3072]{1,0:T(8,128)(2,1)S(1)}, bf16[32,3072]{1,0:T(8,128)(2,1)S(1)}, u32[]{:S(2)}, u32[]{:S(2)}) collective-permute-start(bf16[32,3072]{1,0:T(8,128)(2,1)S(1)} %collective-permute-done.37.refs_6_), channel_id=1, source_target_pairs={{0,4},{2,6},{4,0},{6,2},{8,12},{10,14},{12,8},{14,10},{16,20},{18,... | collective-permute-start | bytes 589832 | tf_op jit(solution)/shard_map/ppermute | solution.py:165
  181.5 6.2 %collective-permute-start.60 = (bf16[32,3072]{1,0:T(8,128)(2,1)S(1)}, bf16[32,3072]{1,0:T(8,128)(2,1)S(1)}, u32[]{:S(2)}, u32[]{:S(2)}) collective-permute-start(bf16[32,3072]{1,0:T(8,128)(2,1)S(1)} %collective-permute-done.52.refs_6_), channel_id=1, source_target_pairs={{0,2},{2,0},{4,6},{6,4},{8,10},{10,8},{12,14},{14,12},{16,18},{18,... | collective-permute-start | bytes 589832 | tf_op jit(solution)/shard_map/ppermute | solution.py:165
  181.6 6.7 %collective-permute-start.44 = (bf16[32,3072]{1,0:T(8,128)(2,1)S(1)}, bf16[32,3072]{1,0:T(8,128)(2,1)S(1)}, u32[]{:S(2)}, u32[]{:S(2)}) collective-permute-start(bf16[32,3072]{1,0:T(8,128)(2,1)S(1)} %collective-permute-done.36.refs_5_), channel_id=1, source_target_pairs={{0,2},{2,0},{4,6},{6,4},{8,10},{10,8},{12,14},{14,12},{16,18},{18,... | collective-permute-start | bytes 589832 | tf_op jit(solution)/shard_map/ppermute | solution.py:165
  185.7 2.7 %collective-permute-start.45 = (bf16[32,3072]{1,0:T(8,128)(2,1)S(1)}, bf16[32,3072]{1,0:T(8,128)(2,1)S(1)}, u32[]{:S(2)}, u32[]{:S(2)}) collective-permute-start(bf16[32,3072]{1,0:T(8,128)(2,1)S(1)} %collective-permute-done.37.refs_6_), channel_id=1, source_target_pairs={{0,2},{2,0},{4,6},{6,4},{8,10},{10,8},{12,14},{14,12},{16,18},{18,... | collective-permute-start | bytes 589832 | tf_op jit(solution)/shard_map/ppermute | solution.py:165
  185.7 3.2 %collective-permute-start.61 = (bf16[32,3072]{1,0:T(8,128)(2,1)S(1)}, bf16[32,3072]{1,0:T(8,128)(2,1)S(1)}, u32[]{:S(2)}, u32[]{:S(2)}) collective-permute-start(bf16[32,3072]{1,0:T(8,128)(2,1)S(1)} %collective-permute-done.53.refs_7_), channel_id=1, source_target_pairs={{0,2},{2,0},{4,6},{6,4},{8,10},{10,8},{12,14},{14,12},{16,18},{18,... | collective-permute-start | bytes 589832 | tf_op jit(solution)/shard_map/ppermute | solution.py:165
  187.8 6.2 %collective-permute-start.46 = (bf16[32,3072]{1,0:T(8,128)(2,1)S(1)}, bf16[32,3072]{1,0:T(8,128)(2,1)S(1)}, u32[]{:S(2)}, u32[]{:S(2)}) collective-permute-start(bf16[32,3072]{1,0:T(8,128)(2,1)S(1)} %collective-permute-done.38.refs_7_), channel_id=1, source_target_pairs={{0,2},{2,0},{4,6},{6,4},{8,10},{10,8},{12,14},{14,12},{16,18},{18,... | collective-permute-start | bytes 589832 | tf_op jit(solution)/shard_map/ppermute | solution.py:165
  187.8 10.9 %collective-permute-start.28 = (bf16[64,1024]{1,0:T(8,128)(2,1)S(1)}, bf16[64,1024]{1,0:T(8,128)(2,1)}, u32[]{:S(2)}, u32[]{:S(2)}) collective-permute-start(bf16[64,1024]{1,0:T(8,128)(2,1)S(1)} %pad_maximum_fusion.refs_0_), channel_id=1, source_target_pairs={{0,2},{2,0},{4,6},{6,4},{8,10},{10,8},{12,14},{14,12},{16,18},{18,... | collective-permute-start | bytes 393224 | tf_op jit(solution)/shard_map/ppermute | solution.py:165
  188.3 10.4 %collective-permute-start.29 = (bf16[64,1024]{1,0:T(8,128)(2,1)}, bf16[64,1024]{1,0:T(8,128)(2,1)}, u32[]{:S(2)}, u32[]{:S(2)}) collective-permute-start(bf16[64,1024]{1,0:T(8,128)(2,1)} %collective-permute-done.25.refs_1_), channel_id=1, source_target_pairs={{0,2},{2,0},{4,6},{6,4},{8,10},{10,8},{12,14},{14,12},{16,18},{18,... | collective-permute-start | bytes 393224 | tf_op jit(solution)/shard_map/ppermute | solution.py:165
  188.4 10.3 %collective-permute-start.30 = (bf16[64,1024]{1,0:T(8,128)(2,1)}, bf16[64,1024]{1,0:T(8,128)(2,1)}, u32[]{:S(2)}, u32[]{:S(2)}) collective-permute-start(bf16[64,1024]{1,0:T(8,128)(2,1)} %collective-permute-done.26.refs_2_), channel_id=1, source_target_pairs={{0,2},{2,0},{4,6},{6,4},{8,10},{10,8},{12,14},{14,12},{16,18},{18,... | collective-permute-start | bytes 393224 | tf_op jit(solution)/shard_map/ppermute | solution.py:165
  189.7 9.0 %collective-permute-start.31 = (bf16[64,1024]{1,0:T(8,128)(2,1)}, bf16[64,1024]{1,0:T(8,128)(2,1)}, u32[]{:S(2)}, u32[]{:S(2)}) collective-permute-start(bf16[64,1024]{1,0:T(8,128)(2,1)} %collective-permute-done.27.refs_3_), channel_id=1, source_target_pairs={{0,2},{2,0},{4,6},{6,4},{8,10},{10,8},{12,14},{14,12},{16,18},{18,... | collective-permute-start | bytes 393224 | tf_op jit(solution)/shard_map/ppermute | solution.py:165
  (37 other events, 802.0 us)
